TPU v7x, 256 devices: a whole 4x4x8 slice. The times are simulated.
256 devices in a mesh: sec: 8 (over z), row: 8 (over y_lo, x), inner: 4 (over y_hi, core).
Axes of the slice: x: 4, y: 4 (y_hi: 2, y_lo: 2; y = y_hi * 2 + y_lo), z: 8, core: 2. Of those that a mesh axis runs over, the one named last changes fastest.
Arguments:
- amplitudes: bfloat16 [1024, 4, 16384], P('row', 'inner'), may hold values from -6 to 6
- hole_ladder: bfloat16 [1024, 1024], P('row'), may hold values from -0.1875 to 0.1875
- bare_integrals: bfloat16 [1024, 4, 16384], P('row', 'inner', 'sec'), may hold values from -6 to 6
- ladder_tiles: bfloat16 [2048, 512, 128], P('sec', 'inner'), may hold values from -0.125 to 0.125
- ladder_source: int32 [2048, 4], P('sec', 'inner'), may hold values from 0 to 127
- ladder_target: int32 [2048, 4], P('sec', 'inner'), may hold values from 0 to 127
- ladder_live: int32 [8, 4], P('sec', 'inner'), may hold values from 64 to 256, as said below
- cycle_tiles: bfloat16 [256, 512, 128], P('sec', 'inner'), may hold values from -0.375 to 0.375
- cycle_source: int32 [256, 4], P('sec', 'inner'), may hold values from 0 to 63
- cycle_target: int32 [256, 4], P('sec', 'inner'), may hold values from 0 to 127
- gap_rows: int32 [1024], P('row'), may hold values from 512 to 2047
- gap_columns: int32 [4, 16384], P('inner', 'sec'), may hold values from 512 to 2047
Outputs:
- updated: bfloat16 [1024, 4, 16384], P('row', 'inner', 'sec')
Inputs may be any that keep to these rules, and one draw needn't show every extreme that they name: Slots from ladder_live on are padding and carry no term; some section and quarter has all 256 slots live in every draw.
All inputs are finite; a program needn't handle non-finite values.
Results may differ from a plain program's by a relative error of at most 0.0095.
Values may be sent and summed in bfloat16 or wider, within the bound.
No kernel may reach another device: no remote copies, remote signals or barrier semaphores. Data moves between devices by JAX's collectives and lax.ppermute only.
A program may use at most 128 MiB of HBM per device.

v0:
```python
import jax
import jax.numpy as jnp
from jax import lax
from jax.sharding import PartitionSpec as P

TILE = 128
TILE_GROUP = 16
PANEL = 2048


def apply_tiles(totals, source_blocks, tiles, sources, targets, live_count, turn_count):

    def one_turn(turn_index, running):
        offset = turn_index * TILE_GROUP
        group_tiles = lax.dynamic_slice_in_dim(tiles, offset, TILE_GROUP, 0)
        group_sources = lax.dynamic_slice_in_dim(sources, offset, TILE_GROUP, 0)
        group_targets = lax.dynamic_slice_in_dim(targets, offset, TILE_GROUP, 0)
        picked = jnp.take(source_blocks, group_sources, axis=1)
        contribution = jnp.einsum(
            "rtk,tkc->rtc", picked, group_tiles, preferred_element_type=jnp.float32
        )
        keep_mask = (offset + jnp.arange(TILE_GROUP) < live_count).astype(jnp.float32)
        contribution = contribution * keep_mask[None, :, None]
        return running.at[:, group_targets].add(contribution)

    return lax.fori_loop(0, turn_count, one_turn, totals)


def per_device(
    amplitudes,
    hole_ladder,
    bare_integrals,
    ladder_tiles,
    ladder_source,
    ladder_target,
    ladder_live,
    cycle_tiles,
    cycle_source,
    cycle_target,
    gap_rows,
    gap_columns,
):
    row_count = amplitudes.shape[0]
    quarter_width = amplitudes.shape[2]
    block_count = quarter_width // TILE
    owned_width = bare_integrals.shape[2]
    own_blocks = amplitudes.reshape(row_count, block_count, TILE)
    gathered_panel = lax.all_gather(amplitudes[:, :, :PANEL], "inner", axis=1, tiled=True)
    panel_blocks = gathered_panel.reshape(row_count, gathered_panel.shape[1] * PANEL // TILE, TILE)
    live_count = ladder_live[0, 0]
    totals = jnp.zeros((row_count, block_count, TILE), jnp.float32)
    totals = apply_tiles(
        totals,
        own_blocks,
        ladder_tiles,
        ladder_source[:, 0],
        ladder_target[:, 0],
        live_count,
        (live_count + TILE_GROUP - 1) // TILE_GROUP,
    )
    cycle_count = cycle_tiles.shape[0]
    totals = apply_tiles(
        totals,
        panel_blocks,
        cycle_tiles,
        cycle_source[:, 0],
        cycle_target[:, 0],
        cycle_count,
        cycle_count // TILE_GROUP,
    )
    partial_sum = totals.reshape(row_count, 1, quarter_width)
    owned_start = lax.axis_index("sec") * owned_width
    joined = lax.psum_scatter(
        partial_sum.astype(jnp.bfloat16), "sec", scatter_dimension=2, tiled=True
    ).astype(jnp.float32)
    owned_amps = lax.dynamic_slice_in_dim(amplitudes, owned_start, owned_width, 2).reshape(
        row_count, owned_width
    )
    hole_term = jnp.dot(
        hole_ladder,
        lax.all_gather(owned_amps, "row", axis=0, tiled=True),
        preferred_element_type=jnp.float32,
    )
    residual = bare_integrals[:, 0, :].astype(jnp.float32) + joined[:, 0, :] + hole_term
    denominator = (gap_rows[:, None] + gap_columns[0][None, :]).astype(jnp.float32) / 1024.0
    updated = (residual / denominator).astype(jnp.bfloat16)
    return updated.reshape(row_count, 1, owned_width)


def solution(mesh):
    in_specs = (
        P("row", "inner", None),
        P("row", None),
        P("row", "inner", "sec"),
        P("sec", "inner", None),
        P("sec", "inner"),
        P("sec", "inner"),
        P("sec", "inner"),
        P("sec", "inner", None),
        P("sec", "inner"),
        P("sec", "inner"),
        P("row"),
        P("inner", "sec"),
    )
    out_specs = P("row", "inner", "sec")
    return jax.shard_map(
        per_device, mesh=mesh, in_specs=in_specs, out_specs=out_specs, check_vma=False
    )
```

profile of v0, /device:TPU:1, one launch (start us, length us, event | category | flops | bytes accessed | tf_op | source)
XLA Modules:
  0.0 270.1 jit_solution(16971075988322931890)
XLA Ops:
  10.3 6.4 %copy.44 = bf16[128,1,16384]{0,2,1:T(8,128)(2,1)} copy(bf16[128,1,16384]{2,0,1:T(8,128)(2,1)} %param.16) | data formatting | bytes 8388608 | tf_op args[0]
  16.7 6.4 %copy.46 = bf16[128,128,128]{2,0,1:T(8,128)(2,1)} copy(bf16[128,128,128]{0,2,1:T(8,128)(2,1)} %bitcast.56) | data formatting | bytes 8388608 | tf_op jit(solution)/shard_map/while | solution.py:26
  23.1 4.4 %broadcast_in_dim.54 = f32[128,128,128]{2,0,1:T(8,128)} broadcast(f32[]{:T(128)} %constant.115.clone.1), dimensions={} | broadcast | bytes 8388612 | tf_op jit(solution)/shard_map/broadcast_in_dim | solution.py:51
  27.5 54.2 %while.23 = (s32[]{:T(128)}, f32[128,128,128]{2,0,1:T(8,128)}, s32[]{:T(128)}, s32[256]{0:T(256)S(1)}, bf16[256,128,128]{2,1,0:T(8,128)(2,1)}, /*index=5*/s32[25...) while((s32[]{:T(128)}, f32[128,128,128]{2,0,1:T(8,128)}, ...), condition=%wide.region_2.3_spmd, body=%wide.region_0.2_spmd.sunk | while | flops 67896520 | bytes 8393495 | solution.py:26
  28.3 2.8 %gather_fusion = bf16[16,128,128]{2,1,0:T(8,128)(2,1)S(1)} fusion(bf16[128,128,128]{2,0,1:T(8,128)(2,1)} %get-tuple-element.380, s32[1024]{0:T(1024)S(1)} %pad_clamp_fusion.4), kind=kCustom, calls=%fused_computation.clone.1 | custom fusion | bytes 1048640 | tf_op jit(solution)/shard_map/while/body/jit(_take)/gather | solution.py:18
  33.1 3.5 %scatter_fusion = f32[128,128,128]{2,0,1:T(8,128)} fusion(f32[128,128,128]{2,0,1:T(8,128)} %get-tuple-element.363, s32[16]{0:T(128)S(1)} %compare_select_fusion.8, f32[16,128,128]{2,1,0:T(8,128)S(1)} %copy.56), kind=kCustom, calls=%fused_computation.2.clone.1 | custom fusion | flops 262144 | bytes 3145792 | tf_op jit(solution)/shard_map/while/body/scatter-add | solution.py:24
  37.3 2.9 %gather_fusion = bf16[16,128,128]{2,1,0:T(8,128)(2,1)S(1)} fusion(bf16[128,128,128]{2,0,1:T(8,128)(2,1)} %get-tuple-element.380, s32[1024]{0:T(1024)S(1)} %pad_clamp_fusion.4), kind=kCustom, calls=%fused_computation.clone.1 | custom fusion | bytes 1048640 | tf_op jit(solution)/shard_map/while/body/jit(_take)/gather | solution.py:18
  42.2 3.4 %scatter_fusion = f32[128,128,128]{2,0,1:T(8,128)} fusion(f32[128,128,128]{2,0,1:T(8,128)} %get-tuple-element.363, s32[16]{0:T(128)S(1)} %compare_select_fusion.8, f32[16,128,128]{2,1,0:T(8,128)S(1)} %copy.56), kind=kCustom, calls=%fused_computation.2.clone.1 | custom fusion | flops 262144 | bytes 3145792 | tf_op jit(solution)/shard_map/while/body/scatter-add | solution.py:24
  46.4 2.8 %gather_fusion = bf16[16,128,128]{2,1,0:T(8,128)(2,1)S(1)} fusion(bf16[128,128,128]{2,0,1:T(8,128)(2,1)} %get-tuple-element.380, s32[1024]{0:T(1024)S(1)} %pad_clamp_fusion.4), kind=kCustom, calls=%fused_computation.clone.1 | custom fusion | bytes 1048640 | tf_op jit(solution)/shard_map/while/body/jit(_take)/gather | solution.py:18
  51.2 3.4 %scatter_fusion = f32[128,128,128]{2,0,1:T(8,128)} fusion(f32[128,128,128]{2,0,1:T(8,128)} %get-tuple-element.363, s32[16]{0:T(128)S(1)} %compare_select_fusion.8, f32[16,128,128]{2,1,0:T(8,128)S(1)} %copy.56), kind=kCustom, calls=%fused_computation.2.clone.1 | custom fusion | flops 262144 | bytes 3145792 | tf_op jit(solution)/shard_map/while/body/scatter-add | solution.py:24
  60.3 3.4 %scatter_fusion = f32[128,128,128]{2,0,1:T(8,128)} fusion(f32[128,128,128]{2,0,1:T(8,128)} %get-tuple-element.363, s32[16]{0:T(128)S(1)} %compare_select_fusion.8, f32[16,128,128]{2,1,0:T(8,128)S(1)} %copy.56), kind=kCustom, calls=%fused_computation.2.clone.1 | custom fusion | flops 262144 | bytes 3145792 | tf_op jit(solution)/shard_map/while/body/scatter-add | solution.py:24
  64.4 2.9 %gather_fusion = bf16[16,128,128]{2,1,0:T(8,128)(2,1)S(1)} fusion(bf16[128,128,128]{2,0,1:T(8,128)(2,1)} %get-tuple-element.380, s32[1024]{0:T(1024)S(1)} %pad_clamp_fusion.4), kind=kCustom, calls=%fused_computation.clone.1 | custom fusion | bytes 1048640 | tf_op jit(solution)/shard_map/while/body/jit(_take)/gather | solution.py:18
  69.3 3.4 %scatter_fusion = f32[128,128,128]{2,0,1:T(8,128)} fusion(f32[128,128,128]{2,0,1:T(8,128)} %get-tuple-element.363, s32[16]{0:T(128)S(1)} %compare_select_fusion.8, f32[16,128,128]{2,1,0:T(8,128)S(1)} %copy.56), kind=kCustom, calls=%fused_computation.2.clone.1 | custom fusion | flops 262144 | bytes 3145792 | tf_op jit(solution)/shard_map/while/body/scatter-add | solution.py:24
  73.4 2.9 %gather_fusion = bf16[16,128,128]{2,1,0:T(8,128)(2,1)S(1)} fusion(bf16[128,128,128]{2,0,1:T(8,128)(2,1)} %get-tuple-element.380, s32[1024]{0:T(1024)S(1)} %pad_clamp_fusion.4), kind=kCustom, calls=%fused_computation.clone.1 | custom fusion | bytes 1048640 | tf_op jit(solution)/shard_map/while/body/jit(_take)/gather | solution.py:18
  78.3 3.4 %scatter_fusion = f32[128,128,128]{2,0,1:T(8,128)} fusion(f32[128,128,128]{2,0,1:T(8,128)} %get-tuple-element.363, s32[16]{0:T(128)S(1)} %compare_select_fusion.8, f32[16,128,128]{2,1,0:T(8,128)S(1)} %copy.56), kind=kCustom, calls=%fused_computation.2.clone.1 | custom fusion | flops 262144 | bytes 3145792 | tf_op jit(solution)/shard_map/while/body/scatter-add | solution.py:24
  81.8 3.1 %copy.47 = bf16[128,4,2048]{0,2,1:T(8,128)(2,1)S(1)} copy(bf16[128,4,2048]{2,0,1:T(8,128)(2,1)} %all-gather.4.cloned.1.call-done) | data formatting | bytes 4194304 | tf_op jit(solution)/shard_map/all_gather | solution.py:48
  84.9 3.0 %copy.49 = bf16[128,64,128]{2,0,1:T(8,128)(2,1)} copy(bf16[128,64,128]{0,2,1:T(8,128)(2,1)S(1)} %bitcast.58) | data formatting | bytes 4194304 | tf_op jit(solution)/shard_map/while | solution.py:26
  87.9 13.5 %while.24 = (s32[]{:T(128)}, f32[128,128,128]{2,0,1:T(8,128)}, s32[32]{0:T(128)S(1)}, bf16[32,128,128]{2,1,0:T(8,128)(2,1)S(1)}, s32[32]{0:T(128)S(1)}, /*index=...) while((s32[]{:T(128)}, f32[128,128,128]{2,0,1:T(8,128)}, s32[32]{0:T(128)S(1)}, ...), condition=%wide.region_5.6_spmd, body=%wide.region_3.5_spmd.sunk | while | flops 67896520 | bytes 8394419 | solution.py:26
  91.2 3.5 %scatter_fusion.1 = f32[128,128,128]{2,0,1:T(8,128)} fusion(f32[128,128,128]{2,0,1:T(8,128)} %get-tuple-element.397, s32[16]{0:T(128)S(1)} %compare_select_fusion.9, f32[16,128,128]{2,1,0:T(8,128)S(1)} %copy.57), kind=kCustom, calls=%fused_computation.3.clone.1 | custom fusion | flops 262144 | bytes 3145792 | tf_op jit(solution)/shard_map/while/body/eval_jaxpr/scatter-add | solution.py:24
  98.0 3.4 %scatter_fusion.1 = f32[128,128,128]{2,0,1:T(8,128)} fusion(f32[128,128,128]{2,0,1:T(8,128)} %get-tuple-element.397, s32[16]{0:T(128)S(1)} %compare_select_fusion.9, f32[16,128,128]{2,1,0:T(8,128)S(1)} %copy.57), kind=kCustom, calls=%fused_computation.3.clone.1 | custom fusion | flops 262144 | bytes 3145792 | tf_op jit(solution)/shard_map/while/body/eval_jaxpr/scatter-add | solution.py:24
  101.4 6.3 %convert_element_type.46 = bf16[128,128,128]{2,0,1:T(8,128)(2,1)} convert(f32[128,128,128]{2,0,1:T(8,128)} %get-tuple-element.158) | non-fusion elementwise | flops 2097152 | bytes 12582912 | tf_op jit(solution)/shard_map/convert_element_type | solution.py:74
  107.7 6.4 %copy.50 = bf16[128,128,128]{0,2,1:T(8,128)(2,1)} copy(bf16[128,128,128]{2,0,1:T(8,128)(2,1)} %convert_element_type.46) | data formatting | bytes 8388608 | tf_op jit(solution)/shard_map/convert_element_type | solution.py:74
  114.5 144.2 %reduce-scatter.2.cloned.1.call-done = bf16[128,1,2048]{0,2,1:T(8,128)(2,1)} async-done(((bf16[128,1,16384]{0,2,1:T(8,128)(2,1)}), bf16[128,1,2048]{0,2,1:T(8,128)(2,1)}) %reduce-scatter.2.cloned.1.call-update) | async-done | bytes 524304 | tf_op jit(solution)/shard_map/reduce_scatter | solution.py:73
  258.7 3.8 %fusion.30 = bf16[128,1,2048]{0,2,1:T(8,128)(2,1)S(1)} fusion(bf16[128,1024]{1,0:T(8,128)(2,1)S(1)} %copy-done, bf16[1024,1,2048]{2,0,1:T(8,128)(2,1)} %all-gather.6.cloned.1.call-done, bf16[128,1,2048]{0,2,1:T(8,128)(2,1)} %reduce-scatter.2.cloned.1.call-done, bf16[128,1,2048]{0,2,1:T(8,128)(2,1)S(1)} %copy.43, s32[2048]{0:T(1024)S(1)} %bitcast.61, ...), kind=kOutput, calls=%fused_computation.38 | convolution fusion | flops 539230208 | bytes 6038016 | tf_op jit(solution)/shard_map/dot_general | solution.py:79
  (72 shorter events, 30.4 us)
Async XLA Ops:
  6.5 252.2 %copy-start = (bf16[128,1024]{1,0:T(8,128)(2,1)S(1)}, bf16[128,1024]{1,0:T(8,128)(2,1)}, u32[]{:S(2)}) copy-start(bf16[128,1024]{1,0:T(8,128)(2,1)} %param.17) | copy-start | bytes 786436
  6.5 75.2 %all-gather.4.cloned.1.call-start = ((), (), s32[]{:S(2)}) async-start(), calls=%async_computation.1 | async-start | bytes 2621440 | tf_op jit(solution)/shard_map/all_gather | solution.py:48
  8.9 105.6 %all-gather.6.cloned.1.call-start = ((), (), s32[]{:S(2)}) async-start(), calls=%async_computation.3 | async-start | bytes 4718592 | tf_op jit(solution)/shard_map/all_gather | solution.py:81
  9.6 249.1 %reduce-scatter.2.cloned.1.call-start = ((), (), s32[]{:S(2)}) async-start(), calls=%async_computation.2 | async-start | bytes 4718592 | tf_op jit(solution)/shard_map/reduce_scatter | solution.py:73
  16.7 10.8 %copy-start.4 = (s32[256,1]{0,1:T(1,128)S(1)}, s32[256,1]{0,1:T(1,128)}, u32[]{:S(2)}) copy-start(s32[256,1]{0,1:T(1,128)} %param.20) | copy-start | bytes 3076
  16.7 10.8 %copy-start.6 = (s32[256,1]{0,1:T(1,128)S(1)}, s32[256,1]{0,1:T(1,128)}, u32[]{:S(2)}) copy-start(s32[256,1]{0,1:T(1,128)} %param.21) | copy-start | bytes 3076
  81.8 6.1 %copy-start.1 = (bf16[32,128,128]{2,1,0:T(8,128)(2,1)S(1)}, bf16[32,128,128]{2,1,0:T(8,128)(2,1)}, u32[]{:S(2)}) copy-start(bf16[32,128,128]{2,1,0:T(8,128)(2,1)} %param.23) | copy-start | bytes 3145732
  81.8 6.1 %copy-start.3 = (s32[32,1]{0,1:T(1,128)S(1)}, s32[32,1]{0,1:T(1,128)}, u32[]{:S(2)}) copy-start(s32[32,1]{0,1:T(1,128)} %param.24) | copy-start | bytes 388
  81.8 6.1 %copy-start.7 = (s32[32,1]{0,1:T(1,128)S(1)}, s32[32,1]{0,1:T(1,128)}, u32[]{:S(2)}) copy-start(s32[32,1]{0,1:T(1,128)} %param.25) | copy-start | bytes 388
  107.7 6.5 %copy-start.2 = (bf16[128,1,2048]{2,0,1:T(8,128)(2,1)S(1)}, bf16[128,1,2048]{2,0,1:T(8,128)(2,1)}, u32[]{:S(2)}) copy-start(bf16[128,1,2048]{2,0,1:T(8,128)(2,1)} %param.18) | copy-start | bytes 1572868
  107.7 151.0 %copy-start.5 = (s32[1,2048]{1,0:T(1,128)S(1)}, s32[1,2048]{1,0:T(1,128)}, u32[]{:S(2)}) copy-start(s32[1,2048]{1,0:T(1,128)} %param.27) | copy-start | bytes 24580
  107.7 151.0 %copy-start.8 = (s32[128]{0:T(128)S(1)}, s32[128]{0:T(128)}, u32[]{:S(2)}) copy-start(s32[128]{0:T(128)} %param.26) | copy-start | bytes 1540
Sparse Core Ops, SparseCore 0:
  9.1 33.3 all-gather.3
  44.3 53.9 all-gather.5
  114.3 144.3 reduce-scatter.1
where the time goes:
time: 273 us; the launch traced here: 270 us
  waiting for transfers between devices  145 us (53%)
  local copies, waits for them, and re-layouts  57.6 us (21%)
  other arithmetic  38.9 us (14%)
  matrix products  14.5 us (5%)
  between operations  13.8 us (5%)
    reduce_scatter x1, waiting for transfers between devices, per_device(): lax.psum_scatter(partial_sum.astype(jnp.bfloat16), 'sec', scatter_dimensi...  144 us
    scatter-add x8, other arithmetic, one_turn(): return running.at[:, group_targets].add(contribution)  27.4 us
    gather x8, local copies, waits for them, and re-layouts, one_turn(): picked = jnp.take(source_blocks, group_sources, axis=1)  21.6 us
    dot_general x8, matrix products, one_turn(): jnp.einsum('rtk,tkc->rtc', picked, group_tiles, preferred_element_type=jn...  10.7 us
    while x2, local copies, waits for them, and re-layouts, apply_tiles(): return lax.fori_loop(0, turn_count, one_turn, totals)  9.36 us
    unnamed x20, local copies, waits for them, and re-layouts  6.68 us
    convert_element_type x1, local copies, waits for them, and re-layouts, per_device(): partial_sum.astype(jnp.bfloat16)  6.43 us
    convert_element_type x1, other arithmetic, per_device(): partial_sum.astype(jnp.bfloat16)  6.3 us
  transfers between devices with their start and end apart: 3, of which 1 were waited for; matrix products, arithmetic and copies ran while one was open for 38% of the time, Pallas kernels for 0%

commit v1 on v0

v1 whole, which is shorter than its diff:
```python
import functools

import jax
import jax.numpy as jnp
from jax import lax
from jax.experimental import pallas as pl
from jax.experimental.pallas import tpu as pltpu
from jax.sharding import PartitionSpec as P


TILE = 128
PANEL = 2048
VMEM = pltpu.VMEM
F32 = jnp.float32
BF16 = jnp.bfloat16


def whole(memory_space=VMEM):
    return pl.BlockSpec(memory_space=memory_space)


def in_hbm(*arrays):
    return tuple(pltpu.with_memory_space_constraint(a, pltpu.HBM) for a in arrays)


def prepare_body(amps, hole, panel, mine, columns, sem):
    wide, narrow = mine.shape[1], columns.shape[1]
    at = pl.multiple_of(lax.axis_index("sec") * wide, wide)
    line = lax.axis_index("row") // 4
    line_at = pl.multiple_of((1 - line) * narrow, narrow)
    copies = [
        pltpu.make_async_copy(amps.at[:, pl.ds(0, panel.shape[1])], panel, sem.at[0]),
        pltpu.make_async_copy(amps.at[:, pl.ds(at, wide)], mine, sem.at[1]),
        pltpu.make_async_copy(hole.at[:, pl.ds(line_at, narrow)], columns, sem.at[2]),
    ]
    for copy in copies:
        copy.start()
    for copy in copies:
        copy.wait()


def prepare(amps, hole, owned):
    rows = amps.shape[0]
    return pl.pallas_call(
        prepare_body,
        out_shape=(
            jax.ShapeDtypeStruct((rows, PANEL), BF16),
            jax.ShapeDtypeStruct((rows, owned), BF16),
            jax.ShapeDtypeStruct((rows, 4 * rows), BF16),
        ),
        in_specs=[whole(pltpu.HBM)] * 2,
        out_specs=[whole()] * 3,
        scratch_shapes=[pltpu.SemaphoreType.DMA((3,))],
        name="prepare",
        compiler_params=pltpu.CompilerParams(vmem_limit_bytes=4 << 20),
        cost_estimate=pl.CostEstimate(flops=0, bytes_accessed=3 << 20, transcendentals=0),
    )(*in_hbm(amps, hole))


def tile_group(turn, unroll, block_of, tiles, acc, into_of):
    products = []
    for k in range(unroll):
        slot = turn * unroll + k
        products.append(jnp.dot(block_of(slot), tiles[slot], preferred_element_type=F32))
    for k in range(unroll):
        acc[into_of(turn * unroll + k)] += products[k]


def ladder_body(
    source_at, target_at, live_at, amps_at, tiles_at, acc,
    source, target, live, amps, tiles, index_sem, amps_sem, tile_sem, *, parts, unroll,
):
    per_part = tiles.shape[0] // parts
    trash = acc.shape[0] - 1
    copies = [
        pltpu.make_async_copy(at, ref, index_sem.at[k])
        for k, (at, ref) in enumerate(
            ((source_at, source), (target_at, target), (live_at, live))
        )
    ]
    pieces = amps_sem.shape[0]
    height = amps.shape[0] // pieces
    for k in range(pieces):
        at = pl.ds(k * height, height)
        copies.append(pltpu.make_async_copy(amps_at.at[at], amps.at[at], amps_sem.at[k]))
    for copy in copies:
        copy.start()

    def tile_copy(part):
        slots = pl.ds(part * per_part, per_part)
        return pltpu.make_async_copy(tiles_at.at[slots], tiles.at[slots], tile_sem.at[part])

    tile_copy(0).start()

    @pl.loop(0, trash // 8)
    def _(block):
        acc[pl.ds(block * 8, 8)] = jnp.zeros((8,) + acc.shape[1:], F32)

    for copy in copies:
        copy.wait()
    for part in range(1, parts):
        tile_copy(part).start()

    def block_of(slot):
        return amps[:, pl.ds(pl.multiple_of(source[slot] * TILE, TILE), TILE)]

    def into_of(slot):
        return jnp.where(slot < live[0], target[slot], trash)

    for part in range(parts):
        tile_copy(part).wait()
        first = part * per_part // unroll
        count = jnp.clip(live[0] - part * per_part, 0, per_part)

        def group(turn, carry):
            tile_group(turn, unroll, block_of, tiles, acc, into_of)
            return carry

        lax.fori_loop(first, first + (count + unroll - 1) // unroll, group, 0)


def ladder(amps, tiles, source, target, live, *, parts=8, unroll=16):
    rows, width = amps.shape
    slots = tiles.shape[0]
    return pl.pallas_call(
        functools.partial(ladder_body, parts=parts, unroll=unroll),
        out_shape=jax.ShapeDtypeStruct((width // TILE + 1, rows, TILE), F32),
        in_specs=[whole(pltpu.HBM)] * 5,
        out_specs=whole(),
        scratch_shapes=[
            pltpu.SMEM(source.shape, jnp.int32),
            pltpu.SMEM(target.shape, jnp.int32),
            pltpu.SMEM(live.shape, jnp.int32),
            VMEM(amps.shape, BF16),
            VMEM(tiles.shape, BF16),
            pltpu.SemaphoreType.DMA((3,)),
            pltpu.SemaphoreType.DMA((4,)),
            pltpu.SemaphoreType.DMA((parts,)),
        ],
        name="ladder",
        compiler_params=pltpu.CompilerParams(vmem_limit_bytes=28 << 20),
        cost_estimate=pl.CostEstimate(
            flops=2 * slots * rows * TILE * TILE, bytes_accessed=12 << 20, transcendentals=0
        ),
    )(*in_hbm(source, target), live, *in_hbm(amps, tiles))


def cycle_body(
    source_at, target_at, _, own, near, far, both, tiles, acc, *rest, n_sec, unroll
):
    *shares, source, target, panels, index_sem, panel_sem = rest
    rows = acc.shape[1]
    per_panel = panels.shape[2] // TILE
    blocks, half, _ = shares[0].shape
    copies = [
        pltpu.make_async_copy(source_at, source, index_sem.at[0]),
        pltpu.make_async_copy(target_at, target, index_sem.at[1]),
    ]
    for k, panel in enumerate((own, near, far, both)):
        copies.append(pltpu.make_async_copy(panel, panels.at[k], panel_sem.at[k]))
    for copy in copies:
        copy.start()
    for copy in copies:
        copy.wait()
    sec, quarter = lax.axis_index("sec"), lax.axis_index("inner")

    def block_of(slot):
        block = source[slot]
        start = pl.multiple_of((block % per_panel) * TILE, TILE)
        return panels[(block // per_panel) ^ quarter, :, pl.ds(start, TILE)]

    def group(turn, carry):
        tile_group(turn, unroll, block_of, tiles, acc, lambda slot: target[slot])
        return carry

    lax.fori_loop(0, tiles.shape[0] // unroll, group, 0)
    for k in range(n_sec):
        chunk = lax.rem(sec + k, n_sec) * blocks
        for u in range(rows // half):
            at = pl.ds(u * half, half)
            shares[u * n_sec + k][...] = acc[pl.ds(chunk, blocks), at].astype(BF16)


def cycle(acc, own, near, far, both, tiles, source, target, *, n_sec, unroll=16):
    blocks = (acc.shape[0] - 1) // n_sec
    rows = acc.shape[1]
    share = jax.ShapeDtypeStruct((blocks, rows // 2, TILE), BF16)
    outs = pl.pallas_call(
        functools.partial(cycle_body, n_sec=n_sec, unroll=unroll),
        out_shape=(jax.ShapeDtypeStruct(acc.shape, F32),) + (share,) * (2 * n_sec),
        in_specs=[whole(pltpu.HBM)] * 2 + [whole()] + [whole(pl.ANY)] * 4 + [whole()],
        out_specs=[whole()] * (1 + 2 * n_sec),
        scratch_shapes=[
            pltpu.SMEM(source.shape, jnp.int32),
            pltpu.SMEM(target.shape, jnp.int32),
            VMEM((4, rows, PANEL), BF16),
            pltpu.SemaphoreType.DMA((2,)),
            pltpu.SemaphoreType.DMA((4,)),
        ],
        input_output_aliases={2: 0},
        name="cycle",
        compiler_params=pltpu.CompilerParams(vmem_limit_bytes=24 << 20),
        cost_estimate=pl.CostEstimate(
            flops=2 * tiles.shape[0] * rows * TILE * TILE, bytes_accessed=6 << 20, transcendentals=0
        ),
    )(*in_hbm(source, target), acc, own, near, far, both, tiles)
    return outs[1 : 1 + n_sec], outs[1 + n_sec :]


def join_body(moving, kept, out):
    out[...] = (moving[...].astype(F32) + kept[...].astype(F32)).astype(out.dtype)


def join(moving, kept):
    return pl.pallas_call(
        join_body,
        out_shape=jax.ShapeDtypeStruct(moving.shape, moving.dtype),
        in_specs=[whole()] * 2,
        out_specs=whole(),
        name="join",
        compiler_params=pltpu.CompilerParams(vmem_limit_bytes=4 << 20),
        cost_estimate=pl.CostEstimate(flops=moving.size, bytes_accessed=3 << 18, transcendentals=0),
    )(moving, kept)


def hole_body(
    hole_at, partner_at, block_0, block_1, block_2, block_3, own_out, partner_out,
    left, line, small_sem, block_sem,
):
    rows = own_out.shape[0]
    depth = left.shape[1]
    line_size = depth // rows
    row = lax.axis_index("row")
    columns = pl.ds(pl.multiple_of((row // line_size) * depth, depth), depth)
    copies = [
        pltpu.make_async_copy(hole_at.at[:, columns], left.at[pl.ds(0, rows)], small_sem.at[0]),
        pltpu.make_async_copy(partner_at, left.at[pl.ds(rows, rows)], small_sem.at[1]),
    ]
    for d, block in enumerate((block_0, block_1, block_2, block_3)):
        at = pl.multiple_of(lax.rem(row + d, line_size) * rows, rows)
        copies.append(pltpu.make_async_copy(block, line.at[pl.ds(at, rows)], block_sem.at[d]))
    for copy in copies:
        copy.start()
    for copy in copies:
        copy.wait()
    step = 256

    @pl.loop(0, line.shape[1] // step)
    def _(turn):
        cols = pl.ds(pl.multiple_of(turn * step, step), step)
        both = jnp.dot(left[...], line[:, cols], preferred_element_type=F32)
        own_out[:, cols] = both[:rows]
        partner_out[:, cols] = both[rows:].astype(partner_out.dtype)


def hole_products(hole, partner, blocks):
    rows, width = blocks[0].shape
    return pl.pallas_call(
        hole_body,
        out_shape=(
            jax.ShapeDtypeStruct((rows, width), F32),
            jax.ShapeDtypeStruct((rows, width), BF16),
        ),
        in_specs=[whole(pltpu.HBM)] + [whole(pl.ANY)] * 5,
        out_specs=[whole(), whole()],
        scratch_shapes=[
            VMEM((2 * rows, partner.shape[1]), BF16),
            VMEM((4 * rows, width), BF16),
            pltpu.SemaphoreType.DMA((2,)),
            pltpu.SemaphoreType.DMA((4,)),
        ],
        name="hole",
        compiler_params=pltpu.CompilerParams(vmem_limit_bytes=10 << 20),
        cost_estimate=pl.CostEstimate(
            flops=2 * 2 * rows * 4 * rows * width, bytes_accessed=4 << 20, transcendentals=0
        ),
    )(*in_hbm(hole), partner, *blocks)


def base_body(
    gap_rows, gap_columns, bare, hole_own, hole_partner, low_own, low_joined, high_own, high_joined,
    out, scale,
):
    half = low_own.shape[1]
    down = jnp.broadcast_to(gap_rows[...].astype(F32), (out.shape[0], out.shape[0])).T
    for b in range(low_own.shape[0]):
        cols = slice(b * TILE, (b + 1) * TILE)
        scale[:, cols] = 1024.0 / (down + gap_columns[:, cols].astype(F32))
        both = bare[:, cols].astype(F32) + hole_own[:, cols] + hole_partner[:, cols].astype(F32)
        for u, own, joined in ((0, low_own, low_joined), (1, high_own, high_joined)):
            at = slice(u * half, (u + 1) * half)
            out[at, cols] = both[at] + own[b].astype(F32) + joined[b].astype(F32)


def base_sum(gap_rows, gap_columns, bare, hole_own, hole_partner, shares):
    rows, width = bare.shape
    out = jax.ShapeDtypeStruct((rows, width), F32)
    return pl.pallas_call(
        base_body,
        out_shape=(out, out),
        in_specs=[whole()] * 9,
        out_specs=[whole()] * 2,
        name="base",
        compiler_params=pltpu.CompilerParams(vmem_limit_bytes=10 << 20),
        cost_estimate=pl.CostEstimate(flops=5 * rows * width, bytes_accessed=4 << 20, transcendentals=0),
    )(gap_rows, gap_columns, bare, hole_own, hole_partner, *shares)


def last_body(base, scale, low, high, out_at, out, sem):
    blocks, half, _ = low.shape
    pieces = sem.shape[0]
    copies = []
    for piece in range(pieces):
        for b in range(piece * blocks // pieces, (piece + 1) * blocks // pieces):
            cols = slice(b * TILE, (b + 1) * TILE)
            for u, joined in ((0, low), (1, high)):
                at = slice(u * half, (u + 1) * half)
                residual = base[at, cols] + joined[b].astype(F32)
                out[at, cols] = (residual * scale[at, cols]).astype(out.dtype)
        width = out.shape[1] // pieces
        part = pl.ds(piece * width, width)
        copies.append(pltpu.make_async_copy(out.at[:, part], out_at.at[:, part], sem.at[piece]))
        copies[-1].start()
    for copy in copies:
        copy.wait()


def last(base, scale, low, high, *, pieces=4):
    rows, width = base.shape
    return pl.pallas_call(
        last_body,
        out_shape=jax.ShapeDtypeStruct((rows, width), BF16),
        in_specs=[whole()] * 4,
        out_specs=whole(pltpu.HBM),
        scratch_shapes=[VMEM((rows, width), BF16), pltpu.SemaphoreType.DMA((pieces,))],
        name="last",
        compiler_params=pltpu.CompilerParams(vmem_limit_bytes=8 << 20),
        cost_estimate=pl.CostEstimate(flops=3 * rows * width, bytes_accessed=3 << 20, transcendentals=0),
    )(base, scale, low, high)


def per_device(
    amplitudes,
    hole_ladder,
    bare_integrals,
    ladder_tiles,
    ladder_source,
    ladder_target,
    ladder_live,
    cycle_tiles,
    cycle_source,
    cycle_target,
    gap_rows,
    gap_columns,
    *,
    n_sec,
):
    rows = amplitudes.shape[0]
    owned = bare_integrals.shape[2]
    amps = amplitudes.reshape(rows, amplitudes.shape[2])

    forward = [(i, (i + 1) % n_sec) for i in range(n_sec)]
    backward = [(i, (i - 1) % n_sec) for i in range(n_sec)]
    core_flip = [(i, i ^ 1) for i in range(4)]
    y_flip = [(i, i ^ 2) for i in range(4)]
    row_flip = [(i, i ^ 4) for i in range(8)]
    x_next = [(i, (i & 4) + (i + 1) % 4) for i in range(8)]
    x_back = [(i, (i & 4) + (i + 3) % 4) for i in range(8)]
    x_over = [(i, (i & 4) + (i + 2) % 4) for i in range(8)]

    panel, mine, columns = prepare(amps, hole_ladder, owned)
    far = lax.ppermute(panel, "inner", y_flip)
    near = lax.ppermute(panel, "inner", core_flip)
    both = lax.ppermute(far, "inner", core_flip)
    behind = lax.ppermute(mine, "row", x_next)
    ahead = lax.ppermute(mine, "row", x_back)
    over = lax.ppermute(mine, "row", x_over)
    partner_columns = lax.ppermute(columns, "row", row_flip)

    acc = ladder(amps, ladder_tiles, ladder_source[:, 0], ladder_target[:, 0], ladder_live[:, 0])
    shares = cycle(
        acc,
        panel,
        near,
        far,
        both,
        cycle_tiles,
        cycle_source[:, 0],
        cycle_target[:, 0],
        n_sec=n_sec,
    )
    hole_own, partner_part = hole_products(
        hole_ladder, partner_columns, (mine, ahead, over, behind)
    )
    hole_partner = lax.ppermute(partner_part, "row", row_flip)

    ends = {}
    for u in range(2):
        reach = (n_sec // 2, n_sec // 2 - 1)
        ways = (("F", forward, reach[u], 1), ("B", backward, reach[1 - u], -1))
        for name, way, hops, sign in ways:
            moving = shares[u][(sign * hops) % n_sec]
            for hop in range(hops - 1, -1, -1):
                moving = lax.ppermute(moving, "sec", way)
                if hop:
                    moving = join(moving, shares[u][(sign * hop) % n_sec])
            ends[f"{name}{u}"] = moving

    base, scale = base_sum(
        gap_rows.reshape(1, rows),
        gap_columns,
        bare_integrals.reshape(rows, owned),
        hole_own,
        hole_partner,
        (shares[0][0], ends["B0"], shares[1][0], ends["F1"]),
    )
    updated = last(base, scale, ends["F0"], ends["B1"])
    return updated.reshape(rows, 1, owned)


def solution(mesh):
    in_specs = (
        P("row", "inner", None),
        P("row", None),
        P("row", "inner", "sec"),
        P("sec", "inner", None),
        P("sec", "inner"),
        P("sec", "inner"),
        P("sec", "inner"),
        P("sec", "inner", None),
        P("sec", "inner"),
        P("sec", "inner"),
        P("row"),
        P("inner", "sec"),
    )
    out_specs = P("row", "inner", "sec")
    return jax.shard_map(
        functools.partial(per_device, n_sec=mesh.shape["sec"]),
        mesh=mesh,
        in_specs=in_specs,
        out_specs=out_specs,
        check_vma=False,
    )
```

time: 273 us -> 85.5 us (0.31)
  the two profiles are of different devices: /device:TPU:1 before, /device:TPU:6 now
where the time goes in v1:
time: 85.5 us; the launch traced here: 85.3 us
  starting transfers between devices  39.6 us (46%)
  waiting for transfers between devices  30.5 us (36%)
  Pallas kernels  14.2 us (17%)
  between operations  1.03 us (1%)
    ppermute x14, starting transfers between devices, per_device(): moving = lax.ppermute(moving, 'sec', way)  29.1 us
    ppermute x14, waiting for transfers between devices, per_device(): moving = lax.ppermute(moving, 'sec', way)  12.1 us
    ppermute x1, waiting for transfers between devices, per_device(): far = lax.ppermute(panel, 'inner', y_flip)  12 us
    ppermute x1, waiting for transfers between devices, per_device(): ahead = lax.ppermute(mine, 'row', x_back)  6.45 us
    pallas_call x1, Pallas kernels, ladder(): pl.pallas_call(functools.partial(ladder_body, parts=parts, unroll=unroll)...  6.01 us
    ppermute x1, starting transfers between devices, per_device(): far = lax.ppermute(panel, 'inner', y_flip)  3.28 us
    pallas_call x1, Pallas kernels, hole_products(): pl.pallas_call(hole_body, out_shape=(jax.ShapeDtypeStruct((rows, width),...  2.91 us
    ppermute x1, starting transfers between devices, per_device(): behind = lax.ppermute(mine, 'row', x_next)  2.17 us
  transfers between devices with their start and end apart: 22, of which 11 were waited for; matrix products, arithmetic and copies ran while one was open for 0% of the time, Pallas kernels for 14%

profile of v1, /device:TPU:6, one launch (start us, length us, event | category | flops | bytes accessed | tf_op | source)
XLA Modules:
  0.0 85.3 jit_solution(8448102421935995340)
XLA Ops:
  0.0 1.2 %prepare.1 = (bf16[128,2048]{1,0:T(8,128)(2,1)S(1)}, bf16[128,2048]{1,0:T(8,128)(2,1)S(1)}, bf16[128,512]{1,0:T(8,128)(2,1)S(1)}) custom-call(bf16[128,16384]{1,0:T(8,128)(2,1)} %bitcast.12, bf16[128,1024]{1,0:T(8,128)(2,1)} %hole_at.1), custom_call_target="tpu_custom_call" | custom-call | bytes 3145728 | tf_op jit(solution)/shard_map/prepare/pallas_call | solution.py:44
  1.3 3.3 %collective-permute-start.6 = (bf16[128,2048]{1,0:T(8,128)(2,1)S(1)}, bf16[128,2048]{1,0:T(8,128)(2,1)S(1)}, u32[]{:S(2)}, u32[]{:S(2)}) collective-permute-start(bf16[128,2048]{1,0:T(8,128)(2,1)S(1)} %get-tuple-element.32.own), channel_id=1, source_target_pairs={{0,2},{1,3},{2,0},{3,1},{4,6},{5,7},{6,4},{7,5},{8,10},{9,11},{10,... | collective-permute-start | bytes 1572872 | tf_op jit(solution)/shard_map/ppermute | solution.py:372
  4.5 12.0 %collective-permute-done.6.far = bf16[128,2048]{1,0:T(8,128)(2,1)S(1)} collective-permute-done((bf16[128,2048]{1,0:T(8,128)(2,1)S(1)}, bf16[128,2048]{1,0:T(8,128)(2,1)S(1)}, u32[]{:S(2)}, u32[]{:S(2)}) %collective-permute-start.6) | collective-permute-done | bytes 524320 | tf_op jit(solution)/shard_map/ppermute | solution.py:372
  18.4 1.6 %collective-permute-start = (bf16[128,512]{1,0:T(8,128)(2,1)S(1)}, bf16[128,512]{1,0:T(8,128)(2,1)S(1)}, u32[]{:S(2)}, u32[]{:S(2)}) collective-permute-start(bf16[128,512]{1,0:T(8,128)(2,1)S(1)} %get-tuple-element.28), channel_id=1, source_target_pairs={{0,16},{4,20},{8,24},{12,28},{16,0},{20,4},{24,8},{28,12},{1,17},{... | collective-permute-start | bytes 393224 | tf_op jit(solution)/shard_map/ppermute | solution.py:378
  20.7 2.2 %collective-permute-start.3 = (bf16[128,2048]{1,0:T(8,128)(2,1)S(1)}, bf16[128,2048]{1,0:T(8,128)(2,1)S(1)}, u32[]{:S(2)}, u32[]{:S(2)}) collective-permute-start(bf16[128,2048]{1,0:T(8,128)(2,1)S(1)} %get-tuple-element.29.block_0), channel_id=1, source_target_pairs={{0,4},{4,8},{8,12},{12,0},{16,20},{20,24},{24,28},{28,16},{1,5},{5... | collective-permute-start | bytes 1572872 | tf_op jit(solution)/shard_map/ppermute | solution.py:375
  22.9 6.0 %ladder.1._ = f32[129,128,128]{2,1,0:T(8,128)S(1)} custom-call(s32[256]{0:T(256)} %bitcast.14, s32[256]{0:T(256)} %bitcast.15, s32[1]{0:T(128)} %bitcast.9.live_at, bf16[128,16384]{1,0:T(8,128)(2,1)} %bitcast.13, bf16[256,128,128]{2,1,0:T(8,128)(2,1)} %tiles_at.1), custom_call_target="tpu_custom_call" | custom-call | flops 1073741824 | bytes 12582912 | tf_op jit(solution)/shard_map/ladder/pallas_call | solution.py:125
  28.9 2.0 %cycle.1 = (f32[129,128,128]{2,1,0:T(8,128)S(1)}, bf16[16,64,128]{2,1,0:T(8,128)(2,1)S(1)}, bf16[16,64,128]{2,1,0:T(8,128)(2,1)S(1)}, bf16[16,64,128]{2,1,0:T(8,...) custom-call(s32[32]{0:T(128)} %bitcast.16, ...), custom_call_target="tpu_custom_call", output_to_operand_aliasing={{0}: (2, {})} | custom-call | flops 134217728 | bytes 6291456 | tf_op jit(solution)/shard_map/cycle/pallas_call | solution.py:188
  30.9 5.9 %collective-permute-start.18 = (bf16[16,64,128]{2,1,0:T(8,128)(2,1)S(1)}, bf16[16,64,128]{2,1,0:T(8,128)(2,1)S(1)}, u32[]{:S(2)}, u32[]{:S(2)}) collective-permute-start(bf16[16,64,128]{2,1,0:T(8,128)(2,1)S(1)} %get-tuple-element.47), channel_id=1, source_target_pairs={{0,224},{32,0},{64,32},{96,64},{128,96},{160,128},{192,160},{224,1... | collective-permute-start | bytes 786440 | tf_op jit(solution)/shard_map/ppermute | solution.py:404
  36.8 6.4 %collective-permute-done.1.block_1 = bf16[128,2048]{1,0:T(8,128)(2,1)S(1)} collective-permute-done((bf16[128,2048]{1,0:T(8,128)(2,1)S(1)}, bf16[128,2048]{1,0:T(8,128)(2,1)S(1)}, u32[]{:S(2)}, u32[]{:S(2)}) %collective-permute-start.1) | collective-permute-done | bytes 524320 | tf_op jit(solution)/shard_map/ppermute | solution.py:376
  43.3 1.9 %collective-permute-start.11 = (bf16[16,64,128]{2,1,0:T(8,128)(2,1)S(1)}, bf16[16,64,128]{2,1,0:T(8,128)(2,1)S(1)}, u32[]{:S(2)}, u32[]{:S(2)}) collective-permute-start(bf16[16,64,128]{2,1,0:T(8,128)(2,1)S(1)} %get-tuple-element.38), channel_id=1, source_target_pairs={{0,32},{32,64},{64,96},{96,128},{128,160},{160,192},{192,224},{224... | collective-permute-start | bytes 786440 | tf_op jit(solution)/shard_map/ppermute | solution.py:404
  45.2 3.9 %collective-permute-start.8 = (bf16[16,64,128]{2,1,0:T(8,128)(2,1)S(1)}, bf16[16,64,128]{2,1,0:T(8,128)(2,1)S(1)}, u32[]{:S(2)}, u32[]{:S(2)}) collective-permute-start(bf16[16,64,128]{2,1,0:T(8,128)(2,1)S(1)} %get-tuple-element.34), channel_id=1, source_target_pairs={{0,224},{32,0},{64,32},{96,64},{128,96},{160,128},{192,160},{224,1... | collective-permute-start | bytes 786440 | tf_op jit(solution)/shard_map/ppermute | solution.py:404
  49.2 2.1 %collective-permute-start.19 = (bf16[16,64,128]{2,1,0:T(8,128)(2,1)S(1)}, bf16[16,64,128]{2,1,0:T(8,128)(2,1)S(1)}, u32[]{:S(2)}, u32[]{:S(2)}) collective-permute-start(bf16[16,64,128]{2,1,0:T(8,128)(2,1)S(1)} %join.17), channel_id=1, source_target_pairs={{0,224},{32,0},{64,32},{96,64},{128,96},{160,128},{192,160},{224,1... | collective-permute-start | bytes 786440 | tf_op jit(solution)/shard_map/ppermute | solution.py:404
  51.7 2.9 %hole.3 = (f32[128,2048]{1,0:T(8,128)S(1)}, bf16[128,2048]{1,0:T(8,128)(2,1)S(1)}) custom-call(bf16[128,1024]{1,0:T(8,128)(2,1)} %hole_at.1, bf16[128,512]{1,0:T(8,128)(2,1)S(1)} %collective-permute-done.partner_at, bf16[128,2048]{1,0:T(8,128)(2,1)S(1)} %get-tuple-element.29.block_0, bf16[128,2048]{1,0:T(8,128)(2,1)S(1)} %collective-permute-done.1.block_1, ...), custom_call_target="tpu_custom_call" | custom-call | flops 536870912 | bytes 4194304 | tf_op jit(solution)/shard_map/hole/pallas_call | solution.py:258
  54.6 1.6 %collective-permute-done.11.moving = bf16[16,64,128]{2,1,0:T(8,128)(2,1)S(1)} collective-permute-done((bf16[16,64,128]{2,1,0:T(8,128)(2,1)S(1)}, bf16[16,64,128]{2,1,0:T(8,128)(2,1)S(1)}, u32[]{:S(2)}, u32[]{:S(2)}) %collective-permute-start.11) | collective-permute-done | bytes 262176 | tf_op jit(solution)/shard_map/ppermute | solution.py:404
  56.5 3.3 %collective-permute-start.9 = (bf16[16,64,128]{2,1,0:T(8,128)(2,1)S(1)}, bf16[16,64,128]{2,1,0:T(8,128)(2,1)S(1)}, u32[]{:S(2)}, u32[]{:S(2)}) collective-permute-start(bf16[16,64,128]{2,1,0:T(8,128)(2,1)S(1)} %join.10), channel_id=1, source_target_pairs={{0,224},{32,0},{64,32},{96,64},{128,96},{160,128},{192,160},{224,1... | collective-permute-start | bytes 786440 | tf_op jit(solution)/shard_map/ppermute | solution.py:404
  59.8 1.6 %collective-permute-start.4 = (bf16[128,2048]{1,0:T(8,128)(2,1)S(1)}, bf16[128,2048]{1,0:T(8,128)(2,1)S(1)}, u32[]{:S(2)}, u32[]{:S(2)}) collective-permute-start(bf16[128,2048]{1,0:T(8,128)(2,1)S(1)} %get-tuple-element.31), channel_id=1, source_target_pairs={{0,16},{4,20},{8,24},{12,28},{16,0},{20,4},{24,8},{28,12},{1,17},{... | collective-permute-start | bytes 1572872 | tf_op jit(solution)/shard_map/ppermute | solution.py:395
  61.5 3.8 %collective-permute-start.20 = (bf16[16,64,128]{2,1,0:T(8,128)(2,1)S(1)}, bf16[16,64,128]{2,1,0:T(8,128)(2,1)S(1)}, u32[]{:S(2)}, u32[]{:S(2)}) collective-permute-start(bf16[16,64,128]{2,1,0:T(8,128)(2,1)S(1)} %join.18), channel_id=1, source_target_pairs={{0,224},{32,0},{64,32},{96,64},{128,96},{160,128},{192,160},{224,1... | collective-permute-start | bytes 786440 | tf_op jit(solution)/shard_map/ppermute | solution.py:404
  65.5 1.1 %collective-permute-done.12.moving = bf16[16,64,128]{2,1,0:T(8,128)(2,1)S(1)} collective-permute-done((bf16[16,64,128]{2,1,0:T(8,128)(2,1)S(1)}, bf16[16,64,128]{2,1,0:T(8,128)(2,1)S(1)}, u32[]{:S(2)}, u32[]{:S(2)}) %collective-permute-start.12) | collective-permute-done | bytes 262176 | tf_op jit(solution)/shard_map/ppermute | solution.py:404
  67.2 3.8 %collective-permute-start.10 = (bf16[16,64,128]{2,1,0:T(8,128)(2,1)S(1)}, bf16[16,64,128]{2,1,0:T(8,128)(2,1)S(1)}, u32[]{:S(2)}, u32[]{:S(2)}) collective-permute-start(bf16[16,64,128]{2,1,0:T(8,128)(2,1)S(1)} %join.11), channel_id=1, source_target_pairs={{0,224},{32,0},{64,32},{96,64},{128,96},{160,128},{192,160},{224,1... | collective-permute-start | bytes 786440 | tf_op jit(solution)/shard_map/ppermute | solution.py:404
  70.9 1.8 %collective-permute-done.20.moving = bf16[16,64,128]{2,1,0:T(8,128)(2,1)S(1)} collective-permute-done((bf16[16,64,128]{2,1,0:T(8,128)(2,1)S(1)}, bf16[16,64,128]{2,1,0:T(8,128)(2,1)S(1)}, u32[]{:S(2)}, u32[]{:S(2)}) %collective-permute-start.20) | collective-permute-done | bytes 262176 | tf_op jit(solution)/shard_map/ppermute | solution.py:404
  72.8 3.8 %collective-permute-start.21 = (bf16[16,64,128]{2,1,0:T(8,128)(2,1)S(1)}, bf16[16,64,128]{2,1,0:T(8,128)(2,1)S(1)}, u32[]{:S(2)}, u32[]{:S(2)}) collective-permute-start(bf16[16,64,128]{2,1,0:T(8,128)(2,1)S(1)} %join.19), channel_id=1, source_target_pairs={{0,224},{32,0},{64,32},{96,64},{128,96},{160,128},{192,160},{224,1... | collective-permute-start | bytes 786440 | tf_op jit(solution)/shard_map/ppermute | solution.py:404
  76.7 1.2 %collective-permute-done.13.high_joined = bf16[16,64,128]{2,1,0:T(8,128)(2,1)S(1)} collective-permute-done((bf16[16,64,128]{2,1,0:T(8,128)(2,1)S(1)}, bf16[16,64,128]{2,1,0:T(8,128)(2,1)S(1)}, u32[]{:S(2)}, u32[]{:S(2)}) %collective-permute-start.13) | collective-permute-done | bytes 262176 | tf_op jit(solution)/shard_map/ppermute | solution.py:404
  78.9 3.8 %collective-permute-done.21.high = bf16[16,64,128]{2,1,0:T(8,128)(2,1)S(1)} collective-permute-done((bf16[16,64,128]{2,1,0:T(8,128)(2,1)S(1)}, bf16[16,64,128]{2,1,0:T(8,128)(2,1)S(1)}, u32[]{:S(2)}, u32[]{:S(2)}) %collective-permute-start.21) | collective-permute-done | bytes 262176 | tf_op jit(solution)/shard_map/ppermute | solution.py:404
  82.6 1.6 %collective-permute-done.17.low = bf16[16,64,128]{2,1,0:T(8,128)(2,1)S(1)} collective-permute-done((bf16[16,64,128]{2,1,0:T(8,128)(2,1)S(1)}, bf16[16,64,128]{2,1,0:T(8,128)(2,1)S(1)}, u32[]{:S(2)}, u32[]{:S(2)}) %collective-permute-start.17) | collective-permute-done | bytes 262176 | tf_op jit(solution)/shard_map/ppermute | solution.py:404
  (44 shorter events, 5.5 us)
Async XLA Ops:
  1.3 15.3 %collective-permute-start.6 = (bf16[128,2048]{1,0:T(8,128)(2,1)S(1)}, bf16[128,2048]{1,0:T(8,128)(2,1)S(1)}, u32[]{:S(2)}, u32[]{:S(2)}) collective-permute-start(bf16[128,2048]{1,0:T(8,128)(2,1)S(1)} %get-tuple-element.32.own), channel_id=1, source_target_pairs={{0,2},{1,3},{2,0},{3,1},{4,6},{5,7},{6,4},{7,5},{8,10},{9,11},{10,... | collective-permute-start | bytes 1572872 | tf_op jit(solution)/shard_map/ppermute | solution.py:372
  4.5 16.1 %collective-permute-start.5 = (bf16[128,2048]{1,0:T(8,128)(2,1)S(1)}, bf16[128,2048]{1,0:T(8,128)(2,1)S(1)}, u32[]{:S(2)}, u32[]{:S(2)}) collective-permute-start(bf16[128,2048]{1,0:T(8,128)(2,1)S(1)} %get-tuple-element.32.own), channel_id=1, source_target_pairs={{0,1},{1,0},{2,3},{3,2},{4,5},{5,4},{6,7},{7,6},{8,9},{9,8},{10,11... | collective-permute-start | bytes 1572872 | tf_op jit(solution)/shard_map/ppermute | solution.py:373
  16.5 12.4 %collective-permute-start.7 = (bf16[128,2048]{1,0:T(8,128)(2,1)S(1)}, bf16[128,2048]{1,0:T(8,128)(2,1)S(1)}, u32[]{:S(2)}, u32[]{:S(2)}) collective-permute-start(bf16[128,2048]{1,0:T(8,128)(2,1)S(1)} %collective-permute-done.6.far), channel_id=1, source_target_pairs={{0,1},{1,0},{2,3},{3,2},{4,5},{5,4},{6,7},{7,6},{8,9},{9,8},{10,11... | collective-permute-start | bytes 1572872 | tf_op jit(solution)/shard_map/ppermute | solution.py:374
  16.5 26.8 %collective-permute-start.1 = (bf16[128,2048]{1,0:T(8,128)(2,1)S(1)}, bf16[128,2048]{1,0:T(8,128)(2,1)S(1)}, u32[]{:S(2)}, u32[]{:S(2)}) collective-permute-start(bf16[128,2048]{1,0:T(8,128)(2,1)S(1)} %get-tuple-element.29.block_0), channel_id=1, source_target_pairs={{0,12},{4,0},{8,4},{12,8},{16,28},{20,16},{24,20},{28,24},{1,13},{... | collective-permute-start | bytes 1572872 | tf_op jit(solution)/shard_map/ppermute | solution.py:376
  17.3 34.1 %collective-permute-start.2 = (bf16[128,2048]{1,0:T(8,128)(2,1)S(1)}, bf16[128,2048]{1,0:T(8,128)(2,1)S(1)}, u32[]{:S(2)}, u32[]{:S(2)}) collective-permute-start(bf16[128,2048]{1,0:T(8,128)(2,1)S(1)} %get-tuple-element.29.block_0), channel_id=1, source_target_pairs={{0,8},{4,12},{8,0},{12,4},{16,24},{20,28},{24,16},{28,20},{1,9},{5... | collective-permute-start | bytes 1572872 | tf_op jit(solution)/shard_map/ppermute | solution.py:377
  18.4 18.4 %collective-permute-start = (bf16[128,512]{1,0:T(8,128)(2,1)S(1)}, bf16[128,512]{1,0:T(8,128)(2,1)S(1)}, u32[]{:S(2)}, u32[]{:S(2)}) collective-permute-start(bf16[128,512]{1,0:T(8,128)(2,1)S(1)} %get-tuple-element.28), channel_id=1, source_target_pairs={{0,16},{4,20},{8,24},{12,28},{16,0},{20,4},{24,8},{28,12},{1,17},{... | collective-permute-start | bytes 393224 | tf_op jit(solution)/shard_map/ppermute | solution.py:378
  20.7 31.0 %collective-permute-start.3 = (bf16[128,2048]{1,0:T(8,128)(2,1)S(1)}, bf16[128,2048]{1,0:T(8,128)(2,1)S(1)}, u32[]{:S(2)}, u32[]{:S(2)}) collective-permute-start(bf16[128,2048]{1,0:T(8,128)(2,1)S(1)} %get-tuple-element.29.block_0), channel_id=1, source_target_pairs={{0,4},{4,8},{8,12},{12,0},{16,20},{20,24},{24,28},{28,16},{1,5},{5... | collective-permute-start | bytes 1572872 | tf_op jit(solution)/shard_map/ppermute | solution.py:375
  28.9 49.4 %copy-start.1 = (bf16[128,1,2048]{2,0,1:T(8,128)(2,1)S(1)}, bf16[128,1,2048]{2,0,1:T(8,128)(2,1)}, u32[]{:S(2)}) copy-start(bf16[128,1,2048]{2,0,1:T(8,128)(2,1)} %param.14) | copy-start | bytes 1572868
  28.9 49.4 %copy-start.2 = (s32[1,2048]{1,0:T(1,128)S(1)}, s32[1,2048]{1,0:T(1,128)}, u32[]{:S(2)}) copy-start(s32[1,2048]{1,0:T(1,128)} %gap_columns.1) | copy-start | bytes 24580
  30.9 14.3 %collective-permute-start.18 = (bf16[16,64,128]{2,1,0:T(8,128)(2,1)S(1)}, bf16[16,64,128]{2,1,0:T(8,128)(2,1)S(1)}, u32[]{:S(2)}, u32[]{:S(2)}) collective-permute-start(bf16[16,64,128]{2,1,0:T(8,128)(2,1)S(1)} %get-tuple-element.47), channel_id=1, source_target_pairs={{0,224},{32,0},{64,32},{96,64},{128,96},{160,128},{192,160},{224,1... | collective-permute-start | bytes 786440 | tf_op jit(solution)/shard_map/ppermute | solution.py:404
  36.8 12.4 %collective-permute-start.14 = (bf16[16,64,128]{2,1,0:T(8,128)(2,1)S(1)}, bf16[16,64,128]{2,1,0:T(8,128)(2,1)S(1)}, u32[]{:S(2)}, u32[]{:S(2)}) collective-permute-start(bf16[16,64,128]{2,1,0:T(8,128)(2,1)S(1)} %get-tuple-element.43), channel_id=1, source_target_pairs={{0,32},{32,64},{64,96},{96,128},{128,160},{160,192},{192,224},{224... | collective-permute-start | bytes 786440 | tf_op jit(solution)/shard_map/ppermute | solution.py:404
  43.3 13.0 %collective-permute-start.11 = (bf16[16,64,128]{2,1,0:T(8,128)(2,1)S(1)}, bf16[16,64,128]{2,1,0:T(8,128)(2,1)S(1)}, u32[]{:S(2)}, u32[]{:S(2)}) collective-permute-start(bf16[16,64,128]{2,1,0:T(8,128)(2,1)S(1)} %get-tuple-element.38), channel_id=1, source_target_pairs={{0,32},{32,64},{64,96},{96,128},{128,160},{160,192},{192,224},{224... | collective-permute-start | bytes 786440 | tf_op jit(solution)/shard_map/ppermute | solution.py:404
  45.2 11.2 %collective-permute-start.8 = (bf16[16,64,128]{2,1,0:T(8,128)(2,1)S(1)}, bf16[16,64,128]{2,1,0:T(8,128)(2,1)S(1)}, u32[]{:S(2)}, u32[]{:S(2)}) collective-permute-start(bf16[16,64,128]{2,1,0:T(8,128)(2,1)S(1)} %get-tuple-element.34), channel_id=1, source_target_pairs={{0,224},{32,0},{64,32},{96,64},{128,96},{160,128},{192,160},{224,1... | collective-permute-start | bytes 786440 | tf_op jit(solution)/shard_map/ppermute | solution.py:404
  49.2 12.2 %collective-permute-start.19 = (bf16[16,64,128]{2,1,0:T(8,128)(2,1)S(1)}, bf16[16,64,128]{2,1,0:T(8,128)(2,1)S(1)}, u32[]{:S(2)}, u32[]{:S(2)}) collective-permute-start(bf16[16,64,128]{2,1,0:T(8,128)(2,1)S(1)} %join.17), channel_id=1, source_target_pairs={{0,224},{32,0},{64,32},{96,64},{128,96},{160,128},{192,160},{224,1... | collective-permute-start | bytes 786440 | tf_op jit(solution)/shard_map/ppermute | solution.py:404
  51.4 13.9 %collective-permute-start.15 = (bf16[16,64,128]{2,1,0:T(8,128)(2,1)S(1)}, bf16[16,64,128]{2,1,0:T(8,128)(2,1)S(1)}, u32[]{:S(2)}, u32[]{:S(2)}) collective-permute-start(bf16[16,64,128]{2,1,0:T(8,128)(2,1)S(1)} %join.14), channel_id=1, source_target_pairs={{0,32},{32,64},{64,96},{96,128},{128,160},{160,192},{192,224},{224... | collective-permute-start | bytes 786440 | tf_op jit(solution)/shard_map/ppermute | solution.py:404
  56.3 10.2 %collective-permute-start.12 = (bf16[16,64,128]{2,1,0:T(8,128)(2,1)S(1)}, bf16[16,64,128]{2,1,0:T(8,128)(2,1)S(1)}, u32[]{:S(2)}, u32[]{:S(2)}) collective-permute-start(bf16[16,64,128]{2,1,0:T(8,128)(2,1)S(1)} %join.12), channel_id=1, source_target_pairs={{0,32},{32,64},{64,96},{96,128},{128,160},{160,192},{192,224},{224... | collective-permute-start | bytes 786440 | tf_op jit(solution)/shard_map/ppermute | solution.py:404
  56.5 10.6 %collective-permute-start.9 = (bf16[16,64,128]{2,1,0:T(8,128)(2,1)S(1)}, bf16[16,64,128]{2,1,0:T(8,128)(2,1)S(1)}, u32[]{:S(2)}, u32[]{:S(2)}) collective-permute-start(bf16[16,64,128]{2,1,0:T(8,128)(2,1)S(1)} %join.10), channel_id=1, source_target_pairs={{0,224},{32,0},{64,32},{96,64},{128,96},{160,128},{192,160},{224,1... | collective-permute-start | bytes 786440 | tf_op jit(solution)/shard_map/ppermute | solution.py:404
  59.8 16.9 %collective-permute-start.4 = (bf16[128,2048]{1,0:T(8,128)(2,1)S(1)}, bf16[128,2048]{1,0:T(8,128)(2,1)S(1)}, u32[]{:S(2)}, u32[]{:S(2)}) collective-permute-start(bf16[128,2048]{1,0:T(8,128)(2,1)S(1)} %get-tuple-element.31), channel_id=1, source_target_pairs={{0,16},{4,20},{8,24},{12,28},{16,0},{20,4},{24,8},{28,12},{1,17},{... | collective-permute-start | bytes 1572872 | tf_op jit(solution)/shard_map/ppermute | solution.py:395
  61.5 11.2 %collective-permute-start.20 = (bf16[16,64,128]{2,1,0:T(8,128)(2,1)S(1)}, bf16[16,64,128]{2,1,0:T(8,128)(2,1)S(1)}, u32[]{:S(2)}, u32[]{:S(2)}) collective-permute-start(bf16[16,64,128]{2,1,0:T(8,128)(2,1)S(1)} %join.18), channel_id=1, source_target_pairs={{0,224},{32,0},{64,32},{96,64},{128,96},{160,128},{192,160},{224,1... | collective-permute-start | bytes 786440 | tf_op jit(solution)/shard_map/ppermute | solution.py:404
  65.4 11.2 %collective-permute-start.16 = (bf16[16,64,128]{2,1,0:T(8,128)(2,1)S(1)}, bf16[16,64,128]{2,1,0:T(8,128)(2,1)S(1)}, u32[]{:S(2)}, u32[]{:S(2)}) collective-permute-start(bf16[16,64,128]{2,1,0:T(8,128)(2,1)S(1)} %join.15), channel_id=1, source_target_pairs={{0,32},{32,64},{64,96},{96,128},{128,160},{160,192},{192,224},{224... | collective-permute-start | bytes 786440 | tf_op jit(solution)/shard_map/ppermute | solution.py:404
  66.6 11.3 %collective-permute-start.13 = (bf16[16,64,128]{2,1,0:T(8,128)(2,1)S(1)}, bf16[16,64,128]{2,1,0:T(8,128)(2,1)S(1)}, u32[]{:S(2)}, u32[]{:S(2)}) collective-permute-start(bf16[16,64,128]{2,1,0:T(8,128)(2,1)S(1)} %join.13), channel_id=1, source_target_pairs={{0,32},{32,64},{64,96},{96,128},{128,160},{160,192},{192,224},{224... | collective-permute-start | bytes 786440 | tf_op jit(solution)/shard_map/ppermute | solution.py:404
  67.2 11.2 %collective-permute-start.10 = (bf16[16,64,128]{2,1,0:T(8,128)(2,1)S(1)}, bf16[16,64,128]{2,1,0:T(8,128)(2,1)S(1)}, u32[]{:S(2)}, u32[]{:S(2)}) collective-permute-start(bf16[16,64,128]{2,1,0:T(8,128)(2,1)S(1)} %join.11), channel_id=1, source_target_pairs={{0,224},{32,0},{64,32},{96,64},{128,96},{160,128},{192,160},{224,1... | collective-permute-start | bytes 786440 | tf_op jit(solution)/shard_map/ppermute | solution.py:404
  72.8 9.9 %collective-permute-start.21 = (bf16[16,64,128]{2,1,0:T(8,128)(2,1)S(1)}, bf16[16,64,128]{2,1,0:T(8,128)(2,1)S(1)}, u32[]{:S(2)}, u32[]{:S(2)}) collective-permute-start(bf16[16,64,128]{2,1,0:T(8,128)(2,1)S(1)} %join.19), channel_id=1, source_target_pairs={{0,224},{32,0},{64,32},{96,64},{128,96},{160,128},{192,160},{224,1... | collective-permute-start | bytes 786440 | tf_op jit(solution)/shard_map/ppermute | solution.py:404
  76.6 7.7 %collective-permute-start.17 = (bf16[16,64,128]{2,1,0:T(8,128)(2,1)S(1)}, bf16[16,64,128]{2,1,0:T(8,128)(2,1)S(1)}, u32[]{:S(2)}, u32[]{:S(2)}) collective-permute-start(bf16[16,64,128]{2,1,0:T(8,128)(2,1)S(1)} %join.16), channel_id=1, source_target_pairs={{0,32},{32,64},{64,96},{96,128},{128,160},{160,192},{192,224},{224... | collective-permute-start | bytes 786440 | tf_op jit(solution)/shard_map/ppermute | solution.py:404
  (2 other events, 55.4 us)

commit v2 on v1

--- a/solution.py
+++ b/solution.py
@@ -223,58 +223,72 @@
     )(moving, kept)
 
 
-def hole_body(
-    hole_at, partner_at, block_0, block_1, block_2, block_3, own_out, partner_out,
-    left, line, small_sem, block_sem,
-):
-    rows = own_out.shape[0]
-    depth = left.shape[1]
-    line_size = depth // rows
-    row = lax.axis_index("row")
-    columns = pl.ds(pl.multiple_of((row // line_size) * depth, depth), depth)
-    copies = [
-        pltpu.make_async_copy(hole_at.at[:, columns], left.at[pl.ds(0, rows)], small_sem.at[0]),
-        pltpu.make_async_copy(partner_at, left.at[pl.ds(rows, rows)], small_sem.at[1]),
-    ]
-    for d, block in enumerate((block_0, block_1, block_2, block_3)):
-        at = pl.multiple_of(lax.rem(row + d, line_size) * rows, rows)
-        copies.append(pltpu.make_async_copy(block, line.at[pl.ds(at, rows)], block_sem.at[d]))
-    for copy in copies:
-        copy.start()
-    for copy in copies:
-        copy.wait()
-    step = 256
-
+def columns_product(left, line, out, *, step=256):
     @pl.loop(0, line.shape[1] // step)
     def _(turn):
         cols = pl.ds(pl.multiple_of(turn * step, step), step)
-        both = jnp.dot(left[...], line[:, cols], preferred_element_type=F32)
-        own_out[:, cols] = both[:rows]
-        partner_out[:, cols] = both[rows:].astype(partner_out.dtype)
-
-
-def hole_products(hole, partner, blocks):
+        product = jnp.dot(left[...], line[:, cols], preferred_element_type=F32)
+        out[:, cols] = product.astype(out.dtype)
+
+
+def partner_body(left, block_0, block_1, block_2, block_3, out, line, sem):
+    rows = out.shape[0]
+    row = lax.axis_index("row")
+    copies = []
+    for d, block in enumerate((block_0, block_1, block_2, block_3)):
+        at = pl.multiple_of(lax.rem(row + d, line.shape[0] // rows) * rows, rows)
+        copies.append(pltpu.make_async_copy(block, line.at[pl.ds(at, rows)], sem.at[d]))
+        copies[-1].start()
+    for copy in copies:
+        copy.wait()
+    columns_product(left, line, out)
+
+
+def partner_product(columns, blocks):
     rows, width = blocks[0].shape
-    return pl.pallas_call(
-        hole_body,
+    depth = columns.shape[1]
+    return pl.pallas_call(
+        partner_body,
         out_shape=(
-            jax.ShapeDtypeStruct((rows, width), F32),
             jax.ShapeDtypeStruct((rows, width), BF16),
-        ),
-        in_specs=[whole(pltpu.HBM)] + [whole(pl.ANY)] * 5,
-        out_specs=[whole(), whole()],
-        scratch_shapes=[
-            VMEM((2 * rows, partner.shape[1]), BF16),
-            VMEM((4 * rows, width), BF16),
-            pltpu.SemaphoreType.DMA((2,)),
-            pltpu.SemaphoreType.DMA((4,)),
-        ],
-        name="hole",
+            jax.ShapeDtypeStruct((depth, width), BF16),
+        ),
+        in_specs=[whole()] + [whole(pl.ANY)] * 4,
+        out_specs=[whole()] * 2,
+        scratch_shapes=[pltpu.SemaphoreType.DMA((4,))],
+        name="partner",
         compiler_params=pltpu.CompilerParams(vmem_limit_bytes=10 << 20),
         cost_estimate=pl.CostEstimate(
-            flops=2 * 2 * rows * 4 * rows * width, bytes_accessed=4 << 20, transcendentals=0
-        ),
-    )(*in_hbm(hole), partner, *blocks)
+            flops=2 * rows * depth * width, bytes_accessed=4 << 20, transcendentals=0
+        ),
+    )(columns, *blocks)
+
+
+def own_body(hole_at, line, out, left, sem):
+    depth = left.shape[1]
+    row = lax.axis_index("row")
+    columns = pl.ds(pl.multiple_of((row // (depth // left.shape[0])) * depth, depth), depth)
+    copy = pltpu.make_async_copy(hole_at.at[:, columns], left, sem)
+    copy.start()
+    copy.wait()
+    columns_product(left, line, out)
+
+
+def own_product(hole, line):
+    rows = hole.shape[0]
+    depth, width = line.shape
+    return pl.pallas_call(
+        own_body,
+        out_shape=jax.ShapeDtypeStruct((rows, width), F32),
+        in_specs=[whole(pltpu.HBM), whole()],
+        out_specs=whole(),
+        scratch_shapes=[VMEM((rows, depth), BF16), pltpu.SemaphoreType.DMA],
+        name="own",
+        compiler_params=pltpu.CompilerParams(vmem_limit_bytes=10 << 20),
+        cost_estimate=pl.CostEstimate(
+            flops=2 * rows * depth * width, bytes_accessed=4 << 20, transcendentals=0
+        ),
+    )(*in_hbm(hole), line)
 
 
 def base_body(
@@ -389,10 +403,9 @@
         cycle_target[:, 0],
         n_sec=n_sec,
     )
-    hole_own, partner_part = hole_products(
-        hole_ladder, partner_columns, (mine, ahead, over, behind)
-    )
+    partner_part, line = partner_product(partner_columns, (mine, ahead, over, behind))
     hole_partner = lax.ppermute(partner_part, "row", row_flip)
+    hole_own = own_product(hole_ladder, line)
 
     ends = {}
     for u in range(2):

time: 85.5 us -> 85.4 us (level)
  waiting for transfers between devices: 30.5 us -> 29.2 us
  Pallas kernels: 14.2 us -> 15.4 us
    ppermute x14, waiting for transfers between devices: 12.1 us -> 10.6 us  [per_device(): moving = lax.ppermute(moving, 'sec', way)]
    pallas_call x1 -> x2, Pallas kernels: 2.91 us -> 4.33 us  [the longest x1 2.52 us: own_product(): pl.pallas_call(own_body, out_shape=jax.ShapeDtypeStruct((rows, width), F3...]
  transfers between devices with their start and end apart: 22 -> 22, of which waited for: 11 -> 9; matrix products, arithmetic and copies ran while one was open for 0% -> 0% of each run, Pallas kernels for 14% -> 16%
where the time goes in v2:
time: 85.4 us; the launch traced here: 85.3 us
  starting transfers between devices  39.6 us (46%)
  waiting for transfers between devices  29.2 us (34%)
  Pallas kernels  15.4 us (18%)
  between operations  1.07 us (1%)
    ppermute x14, starting transfers between devices, per_device(): moving = lax.ppermute(moving, 'sec', way)  29.1 us
    ppermute x1, waiting for transfers between devices, per_device(): far = lax.ppermute(panel, 'inner', y_flip)  12 us
    ppermute x14, waiting for transfers between devices, per_device(): moving = lax.ppermute(moving, 'sec', way)  10.6 us
    ppermute x1, waiting for transfers between devices, per_device(): ahead = lax.ppermute(mine, 'row', x_back)  6.58 us
    pallas_call x1, Pallas kernels, ladder(): pl.pallas_call(functools.partial(ladder_body, parts=parts, unroll=unroll)...  6.01 us
    ppermute x1, starting transfers between devices, per_device(): far = lax.ppermute(panel, 'inner', y_flip)  3.28 us
    pallas_call x1, Pallas kernels, own_product(): pl.pallas_call(own_body, out_shape=jax.ShapeDtypeStruct((rows, width), F3...  2.52 us
    ppermute x1, starting transfers between devices, per_device(): behind = lax.ppermute(mine, 'row', x_next)  2.17 us
  transfers between devices with their start and end apart: 22, of which 9 were waited for; matrix products, arithmetic and copies ran while one was open for 0% of the time, Pallas kernels for 16%

profile of v2, /device:TPU:6, one launch (start us, length us, event | category | flops | bytes accessed | tf_op | source)
XLA Modules:
  0.0 85.3 jit_solution(6736272293861174439)
XLA Ops:
  0.0 1.2 %prepare.1 = (bf16[128,2048]{1,0:T(8,128)(2,1)S(1)}, bf16[128,2048]{1,0:T(8,128)(2,1)S(1)}, bf16[128,512]{1,0:T(8,128)(2,1)S(1)}) custom-call(bf16[128,16384]{1,0:T(8,128)(2,1)} %bitcast.12, bf16[128,1024]{1,0:T(8,128)(2,1)} %hole_at.1), custom_call_target="tpu_custom_call" | custom-call | bytes 3145728 | tf_op jit(solution)/shard_map/prepare/pallas_call | solution.py:44
  1.3 3.3 %collective-permute-start.6 = (bf16[128,2048]{1,0:T(8,128)(2,1)S(1)}, bf16[128,2048]{1,0:T(8,128)(2,1)S(1)}, u32[]{:S(2)}, u32[]{:S(2)}) collective-permute-start(bf16[128,2048]{1,0:T(8,128)(2,1)S(1)} %get-tuple-element.32.own), channel_id=1, source_target_pairs={{0,2},{1,3},{2,0},{3,1},{4,6},{5,7},{6,4},{7,5},{8,10},{9,11},{10,... | collective-permute-start | bytes 1572872 | tf_op jit(solution)/shard_map/ppermute | solution.py:386
  4.5 12.0 %collective-permute-done.6.far = bf16[128,2048]{1,0:T(8,128)(2,1)S(1)} collective-permute-done((bf16[128,2048]{1,0:T(8,128)(2,1)S(1)}, bf16[128,2048]{1,0:T(8,128)(2,1)S(1)}, u32[]{:S(2)}, u32[]{:S(2)}) %collective-permute-start.6) | collective-permute-done | bytes 524320 | tf_op jit(solution)/shard_map/ppermute | solution.py:386
  18.4 1.6 %collective-permute-start = (bf16[128,512]{1,0:T(8,128)(2,1)S(1)}, bf16[128,512]{1,0:T(8,128)(2,1)S(1)}, u32[]{:S(2)}, u32[]{:S(2)}) collective-permute-start(bf16[128,512]{1,0:T(8,128)(2,1)S(1)} %get-tuple-element.28), channel_id=1, source_target_pairs={{0,16},{4,20},{8,24},{12,28},{16,0},{20,4},{24,8},{28,12},{1,17},{... | collective-permute-start | bytes 393224 | tf_op jit(solution)/shard_map/ppermute | solution.py:392
  20.7 2.2 %collective-permute-start.3 = (bf16[128,2048]{1,0:T(8,128)(2,1)S(1)}, bf16[128,2048]{1,0:T(8,128)(2,1)S(1)}, u32[]{:S(2)}, u32[]{:S(2)}) collective-permute-start(bf16[128,2048]{1,0:T(8,128)(2,1)S(1)} %get-tuple-element.29.block_0), channel_id=1, source_target_pairs={{0,4},{4,8},{8,12},{12,0},{16,20},{20,24},{24,28},{28,16},{1,5},{5... | collective-permute-start | bytes 1572872 | tf_op jit(solution)/shard_map/ppermute | solution.py:389
  22.9 6.0 %ladder.1._ = f32[129,128,128]{2,1,0:T(8,128)S(1)} custom-call(s32[256]{0:T(256)} %bitcast.14, s32[256]{0:T(256)} %bitcast.15, s32[1]{0:T(128)} %bitcast.9.live_at, bf16[128,16384]{1,0:T(8,128)(2,1)} %bitcast.13, bf16[256,128,128]{2,1,0:T(8,128)(2,1)} %tiles_at.1), custom_call_target="tpu_custom_call" | custom-call | flops 1073741824 | bytes 12582912 | tf_op jit(solution)/shard_map/ladder/pallas_call | solution.py:125
  28.9 1.8 %cycle.1 = (f32[129,128,128]{2,1,0:T(8,128)S(1)}, bf16[16,64,128]{2,1,0:T(8,128)(2,1)S(1)}, bf16[16,64,128]{2,1,0:T(8,128)(2,1)S(1)}, bf16[16,64,128]{2,1,0:T(8,...) custom-call(s32[32]{0:T(128)} %bitcast.16, ...), custom_call_target="tpu_custom_call", output_to_operand_aliasing={{0}: (2, {})} | custom-call | flops 134217728 | bytes 6291456 | tf_op jit(solution)/shard_map/cycle/pallas_call | solution.py:188
  30.8 5.9 %collective-permute-start.18 = (bf16[16,64,128]{2,1,0:T(8,128)(2,1)S(1)}, bf16[16,64,128]{2,1,0:T(8,128)(2,1)S(1)}, u32[]{:S(2)}, u32[]{:S(2)}) collective-permute-start(bf16[16,64,128]{2,1,0:T(8,128)(2,1)S(1)} %get-tuple-element.47), channel_id=1, source_target_pairs={{0,224},{32,0},{64,32},{96,64},{128,96},{160,128},{192,160},{224,1... | collective-permute-start | bytes 786440 | tf_op jit(solution)/shard_map/ppermute | solution.py:417
  36.7 6.6 %collective-permute-done.1.block_1 = bf16[128,2048]{1,0:T(8,128)(2,1)S(1)} collective-permute-done((bf16[128,2048]{1,0:T(8,128)(2,1)S(1)}, bf16[128,2048]{1,0:T(8,128)(2,1)S(1)}, u32[]{:S(2)}, u32[]{:S(2)}) %collective-permute-start.1) | collective-permute-done | bytes 524320 | tf_op jit(solution)/shard_map/ppermute | solution.py:390
  43.3 1.9 %collective-permute-start.11 = (bf16[16,64,128]{2,1,0:T(8,128)(2,1)S(1)}, bf16[16,64,128]{2,1,0:T(8,128)(2,1)S(1)}, u32[]{:S(2)}, u32[]{:S(2)}) collective-permute-start(bf16[16,64,128]{2,1,0:T(8,128)(2,1)S(1)} %get-tuple-element.38), channel_id=1, source_target_pairs={{0,32},{32,64},{64,96},{96,128},{128,160},{160,192},{192,224},{224... | collective-permute-start | bytes 786440 | tf_op jit(solution)/shard_map/ppermute | solution.py:417
  45.2 3.9 %collective-permute-start.8 = (bf16[16,64,128]{2,1,0:T(8,128)(2,1)S(1)}, bf16[16,64,128]{2,1,0:T(8,128)(2,1)S(1)}, u32[]{:S(2)}, u32[]{:S(2)}) collective-permute-start(bf16[16,64,128]{2,1,0:T(8,128)(2,1)S(1)} %get-tuple-element.34), channel_id=1, source_target_pairs={{0,224},{32,0},{64,32},{96,64},{128,96},{160,128},{192,160},{224,1... | collective-permute-start | bytes 786440 | tf_op jit(solution)/shard_map/ppermute | solution.py:417
  49.2 2.1 %collective-permute-start.19 = (bf16[16,64,128]{2,1,0:T(8,128)(2,1)S(1)}, bf16[16,64,128]{2,1,0:T(8,128)(2,1)S(1)}, u32[]{:S(2)}, u32[]{:S(2)}) collective-permute-start(bf16[16,64,128]{2,1,0:T(8,128)(2,1)S(1)} %join.17), channel_id=1, source_target_pairs={{0,224},{32,0},{64,32},{96,64},{128,96},{160,128},{192,160},{224,1... | collective-permute-start | bytes 786440 | tf_op jit(solution)/shard_map/ppermute | solution.py:417
  51.7 1.8 %partner.1 = (bf16[128,2048]{1,0:T(8,128)(2,1)S(1)}, bf16[512,2048]{1,0:T(8,128)(2,1)S(1)}) custom-call(bf16[128,512]{1,0:T(8,128)(2,1)S(1)} %collective-permute-done.left, bf16[128,2048]{1,0:T(8,128)(2,1)S(1)} %get-tuple-element.29.block_0, bf16[128,2048]{1,0:T(8,128)(2,1)S(1)} %collective-permute-done.1.block_1, ...), custom_call_target="tpu_custom_call" | custom-call | flops 268435456 | bytes 4194304 | tf_op jit(solution)/shard_map/partner/pallas_call | solution.py:250
  53.5 2.7 %collective-permute-done.11.moving = bf16[16,64,128]{2,1,0:T(8,128)(2,1)S(1)} collective-permute-done((bf16[16,64,128]{2,1,0:T(8,128)(2,1)S(1)}, bf16[16,64,128]{2,1,0:T(8,128)(2,1)S(1)}, u32[]{:S(2)}, u32[]{:S(2)}) %collective-permute-start.11) | collective-permute-done | bytes 262176 | tf_op jit(solution)/shard_map/ppermute | solution.py:417
  56.5 3.3 %collective-permute-start.9 = (bf16[16,64,128]{2,1,0:T(8,128)(2,1)S(1)}, bf16[16,64,128]{2,1,0:T(8,128)(2,1)S(1)}, u32[]{:S(2)}, u32[]{:S(2)}) collective-permute-start(bf16[16,64,128]{2,1,0:T(8,128)(2,1)S(1)} %join.10), channel_id=1, source_target_pairs={{0,224},{32,0},{64,32},{96,64},{128,96},{160,128},{192,160},{224,1... | collective-permute-start | bytes 786440 | tf_op jit(solution)/shard_map/ppermute | solution.py:417
  59.8 1.6 %collective-permute-start.4 = (bf16[128,2048]{1,0:T(8,128)(2,1)S(1)}, bf16[128,2048]{1,0:T(8,128)(2,1)S(1)}, u32[]{:S(2)}, u32[]{:S(2)}) collective-permute-start(bf16[128,2048]{1,0:T(8,128)(2,1)S(1)} %get-tuple-element.31), channel_id=1, source_target_pairs={{0,16},{4,20},{8,24},{12,28},{16,0},{20,4},{24,8},{28,12},{1,17},{... | collective-permute-start | bytes 1572872 | tf_op jit(solution)/shard_map/ppermute | solution.py:407
  61.5 3.8 %collective-permute-start.20 = (bf16[16,64,128]{2,1,0:T(8,128)(2,1)S(1)}, bf16[16,64,128]{2,1,0:T(8,128)(2,1)S(1)}, u32[]{:S(2)}, u32[]{:S(2)}) collective-permute-start(bf16[16,64,128]{2,1,0:T(8,128)(2,1)S(1)} %join.18), channel_id=1, source_target_pairs={{0,224},{32,0},{64,32},{96,64},{128,96},{160,128},{192,160},{224,1... | collective-permute-start | bytes 786440 | tf_op jit(solution)/shard_map/ppermute | solution.py:417
  65.5 1.1 %collective-permute-done.12.moving = bf16[16,64,128]{2,1,0:T(8,128)(2,1)S(1)} collective-permute-done((bf16[16,64,128]{2,1,0:T(8,128)(2,1)S(1)}, bf16[16,64,128]{2,1,0:T(8,128)(2,1)S(1)}, u32[]{:S(2)}, u32[]{:S(2)}) %collective-permute-start.12) | collective-permute-done | bytes 262176 | tf_op jit(solution)/shard_map/ppermute | solution.py:417
  67.2 3.8 %collective-permute-start.10 = (bf16[16,64,128]{2,1,0:T(8,128)(2,1)S(1)}, bf16[16,64,128]{2,1,0:T(8,128)(2,1)S(1)}, u32[]{:S(2)}, u32[]{:S(2)}) collective-permute-start(bf16[16,64,128]{2,1,0:T(8,128)(2,1)S(1)} %join.11), channel_id=1, source_target_pairs={{0,224},{32,0},{64,32},{96,64},{128,96},{160,128},{192,160},{224,1... | collective-permute-start | bytes 786440 | tf_op jit(solution)/shard_map/ppermute | solution.py:417
  70.9 1.8 %collective-permute-done.20.moving = bf16[16,64,128]{2,1,0:T(8,128)(2,1)S(1)} collective-permute-done((bf16[16,64,128]{2,1,0:T(8,128)(2,1)S(1)}, bf16[16,64,128]{2,1,0:T(8,128)(2,1)S(1)}, u32[]{:S(2)}, u32[]{:S(2)}) %collective-permute-start.20) | collective-permute-done | bytes 262176 | tf_op jit(solution)/shard_map/ppermute | solution.py:417
  72.8 3.8 %collective-permute-start.21 = (bf16[16,64,128]{2,1,0:T(8,128)(2,1)S(1)}, bf16[16,64,128]{2,1,0:T(8,128)(2,1)S(1)}, u32[]{:S(2)}, u32[]{:S(2)}) collective-permute-start(bf16[16,64,128]{2,1,0:T(8,128)(2,1)S(1)} %join.19), channel_id=1, source_target_pairs={{0,224},{32,0},{64,32},{96,64},{128,96},{160,128},{192,160},{224,1... | collective-permute-start | bytes 786440 | tf_op jit(solution)/shard_map/ppermute | solution.py:417
  76.7 2.5 %own.1.hole_own = f32[128,2048]{1,0:T(8,128)S(1)} custom-call(bf16[128,1024]{1,0:T(8,128)(2,1)} %hole_at.1, bf16[512,2048]{1,0:T(8,128)(2,1)S(1)} %get-tuple-element.30.line), custom_call_target="tpu_custom_call" | custom-call | flops 268435456 | bytes 4194304 | tf_op jit(solution)/shard_map/own/pallas_call | solution.py:280
  79.8 2.8 %collective-permute-done.21.high = bf16[16,64,128]{2,1,0:T(8,128)(2,1)S(1)} collective-permute-done((bf16[16,64,128]{2,1,0:T(8,128)(2,1)S(1)}, bf16[16,64,128]{2,1,0:T(8,128)(2,1)S(1)}, u32[]{:S(2)}, u32[]{:S(2)}) %collective-permute-start.21) | collective-permute-done | bytes 262176 | tf_op jit(solution)/shard_map/ppermute | solution.py:417
  82.6 1.6 %collective-permute-done.17.low = bf16[16,64,128]{2,1,0:T(8,128)(2,1)S(1)} collective-permute-done((bf16[16,64,128]{2,1,0:T(8,128)(2,1)S(1)}, bf16[16,64,128]{2,1,0:T(8,128)(2,1)S(1)}, u32[]{:S(2)}, u32[]{:S(2)}) %collective-permute-start.17) | collective-permute-done | bytes 262176 | tf_op jit(solution)/shard_map/ppermute | solution.py:417
  (45 shorter events, 5.1 us)
Async XLA Ops:
  1.3 15.3 %collective-permute-start.6 = (bf16[128,2048]{1,0:T(8,128)(2,1)S(1)}, bf16[128,2048]{1,0:T(8,128)(2,1)S(1)}, u32[]{:S(2)}, u32[]{:S(2)}) collective-permute-start(bf16[128,2048]{1,0:T(8,128)(2,1)S(1)} %get-tuple-element.32.own), channel_id=1, source_target_pairs={{0,2},{1,3},{2,0},{3,1},{4,6},{5,7},{6,4},{7,5},{8,10},{9,11},{10,... | collective-permute-start | bytes 1572872 | tf_op jit(solution)/shard_map/ppermute | solution.py:386
  4.5 16.1 %collective-permute-start.5 = (bf16[128,2048]{1,0:T(8,128)(2,1)S(1)}, bf16[128,2048]{1,0:T(8,128)(2,1)S(1)}, u32[]{:S(2)}, u32[]{:S(2)}) collective-permute-start(bf16[128,2048]{1,0:T(8,128)(2,1)S(1)} %get-tuple-element.32.own), channel_id=1, source_target_pairs={{0,1},{1,0},{2,3},{3,2},{4,5},{5,4},{6,7},{7,6},{8,9},{9,8},{10,11... | collective-permute-start | bytes 1572872 | tf_op jit(solution)/shard_map/ppermute | solution.py:387
  16.5 12.4 %collective-permute-start.7 = (bf16[128,2048]{1,0:T(8,128)(2,1)S(1)}, bf16[128,2048]{1,0:T(8,128)(2,1)S(1)}, u32[]{:S(2)}, u32[]{:S(2)}) collective-permute-start(bf16[128,2048]{1,0:T(8,128)(2,1)S(1)} %collective-permute-done.6.far), channel_id=1, source_target_pairs={{0,1},{1,0},{2,3},{3,2},{4,5},{5,4},{6,7},{7,6},{8,9},{9,8},{10,11... | collective-permute-start | bytes 1572872 | tf_op jit(solution)/shard_map/ppermute | solution.py:388
  16.5 26.8 %collective-permute-start.1 = (bf16[128,2048]{1,0:T(8,128)(2,1)S(1)}, bf16[128,2048]{1,0:T(8,128)(2,1)S(1)}, u32[]{:S(2)}, u32[]{:S(2)}) collective-permute-start(bf16[128,2048]{1,0:T(8,128)(2,1)S(1)} %get-tuple-element.29.block_0), channel_id=1, source_target_pairs={{0,12},{4,0},{8,4},{12,8},{16,28},{20,16},{24,20},{28,24},{1,13},{... | collective-permute-start | bytes 1572872 | tf_op jit(solution)/shard_map/ppermute | solution.py:390
  17.3 34.1 %collective-permute-start.2 = (bf16[128,2048]{1,0:T(8,128)(2,1)S(1)}, bf16[128,2048]{1,0:T(8,128)(2,1)S(1)}, u32[]{:S(2)}, u32[]{:S(2)}) collective-permute-start(bf16[128,2048]{1,0:T(8,128)(2,1)S(1)} %get-tuple-element.29.block_0), channel_id=1, source_target_pairs={{0,8},{4,12},{8,0},{12,4},{16,24},{20,28},{24,16},{28,20},{1,9},{5... | collective-permute-start | bytes 1572872 | tf_op jit(solution)/shard_map/ppermute | solution.py:391
  18.4 18.3 %collective-permute-start = (bf16[128,512]{1,0:T(8,128)(2,1)S(1)}, bf16[128,512]{1,0:T(8,128)(2,1)S(1)}, u32[]{:S(2)}, u32[]{:S(2)}) collective-permute-start(bf16[128,512]{1,0:T(8,128)(2,1)S(1)} %get-tuple-element.28), channel_id=1, source_target_pairs={{0,16},{4,20},{8,24},{12,28},{16,0},{20,4},{24,8},{28,12},{1,17},{... | collective-permute-start | bytes 393224 | tf_op jit(solution)/shard_map/ppermute | solution.py:392
  20.7 31.0 %collective-permute-start.3 = (bf16[128,2048]{1,0:T(8,128)(2,1)S(1)}, bf16[128,2048]{1,0:T(8,128)(2,1)S(1)}, u32[]{:S(2)}, u32[]{:S(2)}) collective-permute-start(bf16[128,2048]{1,0:T(8,128)(2,1)S(1)} %get-tuple-element.29.block_0), channel_id=1, source_target_pairs={{0,4},{4,8},{8,12},{12,0},{16,20},{20,24},{24,28},{28,16},{1,5},{5... | collective-permute-start | bytes 1572872 | tf_op jit(solution)/shard_map/ppermute | solution.py:389
  30.7 48.5 %copy-start.1 = (bf16[128,1,2048]{2,0,1:T(8,128)(2,1)S(1)}, bf16[128,1,2048]{2,0,1:T(8,128)(2,1)}, u32[]{:S(2)}) copy-start(bf16[128,1,2048]{2,0,1:T(8,128)(2,1)} %param.14) | copy-start | bytes 1572868
  30.8 48.5 %copy-start.2 = (s32[1,2048]{1,0:T(1,128)S(1)}, s32[1,2048]{1,0:T(1,128)}, u32[]{:S(2)}) copy-start(s32[1,2048]{1,0:T(1,128)} %gap_columns.1) | copy-start | bytes 24580
  30.8 14.4 %collective-permute-start.18 = (bf16[16,64,128]{2,1,0:T(8,128)(2,1)S(1)}, bf16[16,64,128]{2,1,0:T(8,128)(2,1)S(1)}, u32[]{:S(2)}, u32[]{:S(2)}) collective-permute-start(bf16[16,64,128]{2,1,0:T(8,128)(2,1)S(1)} %get-tuple-element.47), channel_id=1, source_target_pairs={{0,224},{32,0},{64,32},{96,64},{128,96},{160,128},{192,160},{224,1... | collective-permute-start | bytes 786440 | tf_op jit(solution)/shard_map/ppermute | solution.py:417
  36.7 12.5 %collective-permute-start.14 = (bf16[16,64,128]{2,1,0:T(8,128)(2,1)S(1)}, bf16[16,64,128]{2,1,0:T(8,128)(2,1)S(1)}, u32[]{:S(2)}, u32[]{:S(2)}) collective-permute-start(bf16[16,64,128]{2,1,0:T(8,128)(2,1)S(1)} %get-tuple-element.43), channel_id=1, source_target_pairs={{0,32},{32,64},{64,96},{96,128},{128,160},{160,192},{192,224},{224... | collective-permute-start | bytes 786440 | tf_op jit(solution)/shard_map/ppermute | solution.py:417
  43.3 13.0 %collective-permute-start.11 = (bf16[16,64,128]{2,1,0:T(8,128)(2,1)S(1)}, bf16[16,64,128]{2,1,0:T(8,128)(2,1)S(1)}, u32[]{:S(2)}, u32[]{:S(2)}) collective-permute-start(bf16[16,64,128]{2,1,0:T(8,128)(2,1)S(1)} %get-tuple-element.38), channel_id=1, source_target_pairs={{0,32},{32,64},{64,96},{96,128},{128,160},{160,192},{192,224},{224... | collective-permute-start | bytes 786440 | tf_op jit(solution)/shard_map/ppermute | solution.py:417
  45.2 11.2 %collective-permute-start.8 = (bf16[16,64,128]{2,1,0:T(8,128)(2,1)S(1)}, bf16[16,64,128]{2,1,0:T(8,128)(2,1)S(1)}, u32[]{:S(2)}, u32[]{:S(2)}) collective-permute-start(bf16[16,64,128]{2,1,0:T(8,128)(2,1)S(1)} %get-tuple-element.34), channel_id=1, source_target_pairs={{0,224},{32,0},{64,32},{96,64},{128,96},{160,128},{192,160},{224,1... | collective-permute-start | bytes 786440 | tf_op jit(solution)/shard_map/ppermute | solution.py:417
  49.2 12.2 %collective-permute-start.19 = (bf16[16,64,128]{2,1,0:T(8,128)(2,1)S(1)}, bf16[16,64,128]{2,1,0:T(8,128)(2,1)S(1)}, u32[]{:S(2)}, u32[]{:S(2)}) collective-permute-start(bf16[16,64,128]{2,1,0:T(8,128)(2,1)S(1)} %join.17), channel_id=1, source_target_pairs={{0,224},{32,0},{64,32},{96,64},{128,96},{160,128},{192,160},{224,1... | collective-permute-start | bytes 786440 | tf_op jit(solution)/shard_map/ppermute | solution.py:417
  51.4 13.9 %collective-permute-start.15 = (bf16[16,64,128]{2,1,0:T(8,128)(2,1)S(1)}, bf16[16,64,128]{2,1,0:T(8,128)(2,1)S(1)}, u32[]{:S(2)}, u32[]{:S(2)}) collective-permute-start(bf16[16,64,128]{2,1,0:T(8,128)(2,1)S(1)} %join.14), channel_id=1, source_target_pairs={{0,32},{32,64},{64,96},{96,128},{128,160},{160,192},{192,224},{224... | collective-permute-start | bytes 786440 | tf_op jit(solution)/shard_map/ppermute | solution.py:417
  56.3 10.2 %collective-permute-start.12 = (bf16[16,64,128]{2,1,0:T(8,128)(2,1)S(1)}, bf16[16,64,128]{2,1,0:T(8,128)(2,1)S(1)}, u32[]{:S(2)}, u32[]{:S(2)}) collective-permute-start(bf16[16,64,128]{2,1,0:T(8,128)(2,1)S(1)} %join.12), channel_id=1, source_target_pairs={{0,32},{32,64},{64,96},{96,128},{128,160},{160,192},{192,224},{224... | collective-permute-start | bytes 786440 | tf_op jit(solution)/shard_map/ppermute | solution.py:417
  56.5 10.6 %collective-permute-start.9 = (bf16[16,64,128]{2,1,0:T(8,128)(2,1)S(1)}, bf16[16,64,128]{2,1,0:T(8,128)(2,1)S(1)}, u32[]{:S(2)}, u32[]{:S(2)}) collective-permute-start(bf16[16,64,128]{2,1,0:T(8,128)(2,1)S(1)} %join.10), channel_id=1, source_target_pairs={{0,224},{32,0},{64,32},{96,64},{128,96},{160,128},{192,160},{224,1... | collective-permute-start | bytes 786440 | tf_op jit(solution)/shard_map/ppermute | solution.py:417
  59.8 19.4 %collective-permute-start.4 = (bf16[128,2048]{1,0:T(8,128)(2,1)S(1)}, bf16[128,2048]{1,0:T(8,128)(2,1)S(1)}, u32[]{:S(2)}, u32[]{:S(2)}) collective-permute-start(bf16[128,2048]{1,0:T(8,128)(2,1)S(1)} %get-tuple-element.31), channel_id=1, source_target_pairs={{0,16},{4,20},{8,24},{12,28},{16,0},{20,4},{24,8},{28,12},{1,17},{... | collective-permute-start | bytes 1572872 | tf_op jit(solution)/shard_map/ppermute | solution.py:407
  61.5 11.2 %collective-permute-start.20 = (bf16[16,64,128]{2,1,0:T(8,128)(2,1)S(1)}, bf16[16,64,128]{2,1,0:T(8,128)(2,1)S(1)}, u32[]{:S(2)}, u32[]{:S(2)}) collective-permute-start(bf16[16,64,128]{2,1,0:T(8,128)(2,1)S(1)} %join.18), channel_id=1, source_target_pairs={{0,224},{32,0},{64,32},{96,64},{128,96},{160,128},{192,160},{224,1... | collective-permute-start | bytes 786440 | tf_op jit(solution)/shard_map/ppermute | solution.py:417
  65.4 11.2 %collective-permute-start.16 = (bf16[16,64,128]{2,1,0:T(8,128)(2,1)S(1)}, bf16[16,64,128]{2,1,0:T(8,128)(2,1)S(1)}, u32[]{:S(2)}, u32[]{:S(2)}) collective-permute-start(bf16[16,64,128]{2,1,0:T(8,128)(2,1)S(1)} %join.15), channel_id=1, source_target_pairs={{0,32},{32,64},{64,96},{96,128},{128,160},{160,192},{192,224},{224... | collective-permute-start | bytes 786440 | tf_op jit(solution)/shard_map/ppermute | solution.py:417
  66.6 12.6 %collective-permute-start.13 = (bf16[16,64,128]{2,1,0:T(8,128)(2,1)S(1)}, bf16[16,64,128]{2,1,0:T(8,128)(2,1)S(1)}, u32[]{:S(2)}, u32[]{:S(2)}) collective-permute-start(bf16[16,64,128]{2,1,0:T(8,128)(2,1)S(1)} %join.13), channel_id=1, source_target_pairs={{0,32},{32,64},{64,96},{96,128},{128,160},{160,192},{192,224},{224... | collective-permute-start | bytes 786440 | tf_op jit(solution)/shard_map/ppermute | solution.py:417
  67.2 12.1 %collective-permute-start.10 = (bf16[16,64,128]{2,1,0:T(8,128)(2,1)S(1)}, bf16[16,64,128]{2,1,0:T(8,128)(2,1)S(1)}, u32[]{:S(2)}, u32[]{:S(2)}) collective-permute-start(bf16[16,64,128]{2,1,0:T(8,128)(2,1)S(1)} %join.11), channel_id=1, source_target_pairs={{0,224},{32,0},{64,32},{96,64},{128,96},{160,128},{192,160},{224,1... | collective-permute-start | bytes 786440 | tf_op jit(solution)/shard_map/ppermute | solution.py:417
  72.8 9.9 %collective-permute-start.21 = (bf16[16,64,128]{2,1,0:T(8,128)(2,1)S(1)}, bf16[16,64,128]{2,1,0:T(8,128)(2,1)S(1)}, u32[]{:S(2)}, u32[]{:S(2)}) collective-permute-start(bf16[16,64,128]{2,1,0:T(8,128)(2,1)S(1)} %join.19), channel_id=1, source_target_pairs={{0,224},{32,0},{64,32},{96,64},{128,96},{160,128},{192,160},{224,1... | collective-permute-start | bytes 786440 | tf_op jit(solution)/shard_map/ppermute | solution.py:417
  76.6 7.7 %collective-permute-start.17 = (bf16[16,64,128]{2,1,0:T(8,128)(2,1)S(1)}, bf16[16,64,128]{2,1,0:T(8,128)(2,1)S(1)}, u32[]{:S(2)}, u32[]{:S(2)}) collective-permute-start(bf16[16,64,128]{2,1,0:T(8,128)(2,1)S(1)} %join.16), channel_id=1, source_target_pairs={{0,32},{32,64},{64,96},{96,128},{128,160},{160,192},{192,224},{224... | collective-permute-start | bytes 786440 | tf_op jit(solution)/shard_map/ppermute | solution.py:417
  (2 other events, 54.5 us)

commit v3 on v2

--- a/solution.py
+++ b/solution.py
@@ -23,15 +23,20 @@
     return tuple(pltpu.with_memory_space_constraint(a, pltpu.HBM) for a in arrays)
 
 
-def prepare_body(amps, hole, panel, mine, columns, sem):
+def panel_body(amps, panel, sem):
+    copy = pltpu.make_async_copy(amps.at[:, pl.ds(0, panel.shape[1])], panel, sem)
+    copy.start()
+    copy.wait()
+
+
+def owned_body(amps, hole, mine, columns, sem):
     wide, narrow = mine.shape[1], columns.shape[1]
     at = pl.multiple_of(lax.axis_index("sec") * wide, wide)
     line = lax.axis_index("row") // 4
     line_at = pl.multiple_of((1 - line) * narrow, narrow)
     copies = [
-        pltpu.make_async_copy(amps.at[:, pl.ds(0, panel.shape[1])], panel, sem.at[0]),
-        pltpu.make_async_copy(amps.at[:, pl.ds(at, wide)], mine, sem.at[1]),
-        pltpu.make_async_copy(hole.at[:, pl.ds(line_at, narrow)], columns, sem.at[2]),
+        pltpu.make_async_copy(amps.at[:, pl.ds(at, wide)], mine, sem.at[0]),
+        pltpu.make_async_copy(hole.at[:, pl.ds(line_at, narrow)], columns, sem.at[1]),
     ]
     for copy in copies:
         copy.start()
@@ -39,22 +44,19 @@
         copy.wait()
 
 
-def prepare(amps, hole, owned):
-    rows = amps.shape[0]
-    return pl.pallas_call(
-        prepare_body,
-        out_shape=(
-            jax.ShapeDtypeStruct((rows, PANEL), BF16),
-            jax.ShapeDtypeStruct((rows, owned), BF16),
-            jax.ShapeDtypeStruct((rows, 4 * rows), BF16),
-        ),
-        in_specs=[whole(pltpu.HBM)] * 2,
-        out_specs=[whole()] * 3,
-        scratch_shapes=[pltpu.SemaphoreType.DMA((3,))],
-        name="prepare",
+def picked(body, widths, *arrays):
+    rows = arrays[0].shape[0]
+    out = [jax.ShapeDtypeStruct((rows, width), BF16) for width in widths]
+    sems = () if len(widths) == 1 else (len(widths),)
+    return pl.pallas_call(
+        body,
+        out_shape=out,
+        in_specs=[whole(pltpu.HBM)] * len(arrays),
+        out_specs=[whole()] * len(out),
+        scratch_shapes=[pltpu.SemaphoreType.DMA(sems)],
         compiler_params=pltpu.CompilerParams(vmem_limit_bytes=4 << 20),
-        cost_estimate=pl.CostEstimate(flops=0, bytes_accessed=3 << 20, transcendentals=0),
-    )(*in_hbm(amps, hole))
+        cost_estimate=pl.CostEstimate(flops=0, bytes_accessed=2 << 20, transcendentals=0),
+    )(*in_hbm(*arrays))
 
 
 def tile_group(turn, unroll, block_of, tiles, acc, into_of):
@@ -119,7 +121,7 @@
         lax.fori_loop(first, first + (count + unroll - 1) // unroll, group, 0)
 
 
-def ladder(amps, tiles, source, target, live, *, parts=8, unroll=16):
+def ladder(amps, tiles, source, target, live, *, parts=8, unroll=32):
     rows, width = amps.shape
     slots = tiles.shape[0]
     return pl.pallas_call(
@@ -181,7 +183,7 @@
             shares[u * n_sec + k][...] = acc[pl.ds(chunk, blocks), at].astype(BF16)
 
 
-def cycle(acc, own, near, far, both, tiles, source, target, *, n_sec, unroll=16):
+def cycle(acc, own, near, far, both, tiles, source, target, *, n_sec, unroll=32):
     blocks = (acc.shape[0] - 1) // n_sec
     rows = acc.shape[1]
     share = jax.ShapeDtypeStruct((blocks, rows // 2, TILE), BF16)
@@ -382,7 +384,8 @@
     x_back = [(i, (i & 4) + (i + 3) % 4) for i in range(8)]
     x_over = [(i, (i & 4) + (i + 2) % 4) for i in range(8)]
 
-    panel, mine, columns = prepare(amps, hole_ladder, owned)
+    (panel,) = picked(panel_body, (PANEL,), amps)
+    mine, columns = picked(owned_body, (owned, 4 * rows), amps, hole_ladder)
     far = lax.ppermute(panel, "inner", y_flip)
     near = lax.ppermute(panel, "inner", core_flip)
     both = lax.ppermute(far, "inner", core_flip)

time: 85.4 us -> 86.4 us (1.012)
    pallas_call x1 -> x2, Pallas kernels: 1.25 us -> 2.13 us  [picked(): pl.pallas_call(body, out_shape=out, in_specs=[whole(pltpu.HBM)] * len(arr...]
where the time goes in v3:
time: 86.4 us; the launch traced here: 86.3 us
  starting transfers between devices  39.5 us (46%)
  waiting for transfers between devices  29.6 us (34%)
  Pallas kernels  16.1 us (19%)
  between operations  1.08 us (1%)
    ppermute x14, starting transfers between devices, per_device(): moving = lax.ppermute(moving, 'sec', way)  28.9 us
    ppermute x1, waiting for transfers between devices, per_device(): far = lax.ppermute(panel, 'inner', y_flip)  12 us
    ppermute x14, waiting for transfers between devices, per_device(): moving = lax.ppermute(moving, 'sec', way)  10.8 us
    ppermute x1, waiting for transfers between devices, per_device(): ahead = lax.ppermute(mine, 'row', x_back)  6.85 us
    pallas_call x1, Pallas kernels, ladder(): pl.pallas_call(functools.partial(ladder_body, parts=parts, unroll=unroll)...  5.9 us
    ppermute x1, starting transfers between devices, per_device(): far = lax.ppermute(panel, 'inner', y_flip)  3.28 us
    pallas_call x1, Pallas kernels, own_product(): pl.pallas_call(own_body, out_shape=jax.ShapeDtypeStruct((rows, width), F3...  2.52 us
    ppermute x1, starting transfers between devices, per_device(): behind = lax.ppermute(mine, 'row', x_next)  2.17 us
  transfers between devices with their start and end apart: 22, of which 9 were waited for; matrix products, arithmetic and copies ran while one was open for 0% of the time, Pallas kernels for 16%

profile of v3, /device:TPU:6, one launch (start us, length us, event | category | flops | bytes accessed | tf_op | source)
XLA Modules:
  0.0 86.3 jit_solution(15646816675732932883)
XLA Ops:
  1.1 3.3 %collective-permute-start.6 = (bf16[128,2048]{1,0:T(8,128)(2,1)S(1)}, bf16[128,2048]{1,0:T(8,128)(2,1)S(1)}, u32[]{:S(2)}, u32[]{:S(2)}) collective-permute-start(bf16[128,2048]{1,0:T(8,128)(2,1)S(1)} %shard_map.119.own), channel_id=1, source_target_pairs={{0,2},{1,3},{2,0},{3,1},{4,6},{5,7},{6,4},{7,5},{8,10},{9,11},{10,... | collective-permute-start | bytes 1572872 | tf_op jit(solution)/shard_map/ppermute | solution.py:389
  4.3 12.0 %collective-permute-done.6.far = bf16[128,2048]{1,0:T(8,128)(2,1)S(1)} collective-permute-done((bf16[128,2048]{1,0:T(8,128)(2,1)S(1)}, bf16[128,2048]{1,0:T(8,128)(2,1)S(1)}, u32[]{:S(2)}, u32[]{:S(2)}) %collective-permute-start.6) | collective-permute-done | bytes 524320 | tf_op jit(solution)/shard_map/ppermute | solution.py:389
  16.3 1.1 %shard_map.118 = (bf16[128,2048]{1,0:T(8,128)(2,1)S(1)}, bf16[128,512]{1,0:T(8,128)(2,1)S(1)}) custom-call(bf16[128,16384]{1,0:T(8,128)(2,1)} %bitcast.13, bf16[128,1024]{1,0:T(8,128)(2,1)} %hole_at.1), custom_call_target="tpu_custom_call" | custom-call | bytes 2097152 | tf_op jit(solution)/shard_map/pallas_call | solution.py:51
  19.4 1.6 %collective-permute-start = (bf16[128,512]{1,0:T(8,128)(2,1)S(1)}, bf16[128,512]{1,0:T(8,128)(2,1)S(1)}, u32[]{:S(2)}, u32[]{:S(2)}) collective-permute-start(bf16[128,512]{1,0:T(8,128)(2,1)S(1)} %get-tuple-element.27), channel_id=1, source_target_pairs={{0,16},{4,20},{8,24},{12,28},{16,0},{20,4},{24,8},{28,12},{1,17},{... | collective-permute-start | bytes 393224 | tf_op jit(solution)/shard_map/ppermute | solution.py:395
  21.7 2.2 %collective-permute-start.3 = (bf16[128,2048]{1,0:T(8,128)(2,1)S(1)}, bf16[128,2048]{1,0:T(8,128)(2,1)S(1)}, u32[]{:S(2)}, u32[]{:S(2)}) collective-permute-start(bf16[128,2048]{1,0:T(8,128)(2,1)S(1)} %get-tuple-element.28.block_0), channel_id=1, source_target_pairs={{0,4},{4,8},{8,12},{12,0},{16,20},{20,24},{24,28},{28,16},{1,5},{5... | collective-permute-start | bytes 1572872 | tf_op jit(solution)/shard_map/ppermute | solution.py:392
  23.8 5.9 %ladder.1._ = f32[129,128,128]{2,1,0:T(8,128)S(1)} custom-call(s32[256]{0:T(256)} %bitcast.15, s32[256]{0:T(256)} %bitcast.16, s32[1]{0:T(128)} %bitcast.9.live_at, bf16[128,16384]{1,0:T(8,128)(2,1)} %bitcast.14, bf16[256,128,128]{2,1,0:T(8,128)(2,1)} %tiles_at.1), custom_call_target="tpu_custom_call" | custom-call | flops 1073741824 | bytes 12582912 | tf_op jit(solution)/shard_map/ladder/pallas_call | solution.py:127
  29.8 1.7 %cycle.1 = (f32[129,128,128]{2,1,0:T(8,128)S(1)}, bf16[16,64,128]{2,1,0:T(8,128)(2,1)S(1)}, bf16[16,64,128]{2,1,0:T(8,128)(2,1)S(1)}, bf16[16,64,128]{2,1,0:T(8,...) custom-call(s32[32]{0:T(128)} %bitcast.17, ...), custom_call_target="tpu_custom_call", output_to_operand_aliasing={{0}: (2, {})} | custom-call | flops 134217728 | bytes 6291456 | tf_op jit(solution)/shard_map/cycle/pallas_call | solution.py:190
  31.5 5.9 %collective-permute-start.18 = (bf16[16,64,128]{2,1,0:T(8,128)(2,1)S(1)}, bf16[16,64,128]{2,1,0:T(8,128)(2,1)S(1)}, u32[]{:S(2)}, u32[]{:S(2)}) collective-permute-start(bf16[16,64,128]{2,1,0:T(8,128)(2,1)S(1)} %get-tuple-element.45), channel_id=1, source_target_pairs={{0,224},{32,0},{64,32},{96,64},{128,96},{160,128},{192,160},{224,1... | collective-permute-start | bytes 786440 | tf_op jit(solution)/shard_map/ppermute | solution.py:420
  37.4 6.9 %collective-permute-done.1.block_1 = bf16[128,2048]{1,0:T(8,128)(2,1)S(1)} collective-permute-done((bf16[128,2048]{1,0:T(8,128)(2,1)S(1)}, bf16[128,2048]{1,0:T(8,128)(2,1)S(1)}, u32[]{:S(2)}, u32[]{:S(2)}) %collective-permute-start.1) | collective-permute-done | bytes 524320 | tf_op jit(solution)/shard_map/ppermute | solution.py:393
  44.3 1.9 %collective-permute-start.11 = (bf16[16,64,128]{2,1,0:T(8,128)(2,1)S(1)}, bf16[16,64,128]{2,1,0:T(8,128)(2,1)S(1)}, u32[]{:S(2)}, u32[]{:S(2)}) collective-permute-start(bf16[16,64,128]{2,1,0:T(8,128)(2,1)S(1)} %get-tuple-element.36), channel_id=1, source_target_pairs={{0,32},{32,64},{64,96},{96,128},{128,160},{160,192},{192,224},{224... | collective-permute-start | bytes 786440 | tf_op jit(solution)/shard_map/ppermute | solution.py:420
  46.2 3.9 %collective-permute-start.8 = (bf16[16,64,128]{2,1,0:T(8,128)(2,1)S(1)}, bf16[16,64,128]{2,1,0:T(8,128)(2,1)S(1)}, u32[]{:S(2)}, u32[]{:S(2)}) collective-permute-start(bf16[16,64,128]{2,1,0:T(8,128)(2,1)S(1)} %get-tuple-element.32), channel_id=1, source_target_pairs={{0,224},{32,0},{64,32},{96,64},{128,96},{160,128},{192,160},{224,1... | collective-permute-start | bytes 786440 | tf_op jit(solution)/shard_map/ppermute | solution.py:420
  50.2 2.1 %collective-permute-start.19 = (bf16[16,64,128]{2,1,0:T(8,128)(2,1)S(1)}, bf16[16,64,128]{2,1,0:T(8,128)(2,1)S(1)}, u32[]{:S(2)}, u32[]{:S(2)}) collective-permute-start(bf16[16,64,128]{2,1,0:T(8,128)(2,1)S(1)} %join.17), channel_id=1, source_target_pairs={{0,224},{32,0},{64,32},{96,64},{128,96},{160,128},{192,160},{224,1... | collective-permute-start | bytes 786440 | tf_op jit(solution)/shard_map/ppermute | solution.py:420
  52.5 1.8 %partner.1 = (bf16[128,2048]{1,0:T(8,128)(2,1)S(1)}, bf16[512,2048]{1,0:T(8,128)(2,1)S(1)}) custom-call(bf16[128,512]{1,0:T(8,128)(2,1)S(1)} %collective-permute-done.left, bf16[128,2048]{1,0:T(8,128)(2,1)S(1)} %get-tuple-element.28.block_0, bf16[128,2048]{1,0:T(8,128)(2,1)S(1)} %collective-permute-done.1.block_1, ...), custom_call_target="tpu_custom_call" | custom-call | flops 268435456 | bytes 4194304 | tf_op jit(solution)/shard_map/partner/pallas_call | solution.py:252
  54.3 3.0 %collective-permute-done.11.moving = bf16[16,64,128]{2,1,0:T(8,128)(2,1)S(1)} collective-permute-done((bf16[16,64,128]{2,1,0:T(8,128)(2,1)S(1)}, bf16[16,64,128]{2,1,0:T(8,128)(2,1)S(1)}, u32[]{:S(2)}, u32[]{:S(2)}) %collective-permute-start.11) | collective-permute-done | bytes 262176 | tf_op jit(solution)/shard_map/ppermute | solution.py:420
  57.5 3.3 %collective-permute-start.9 = (bf16[16,64,128]{2,1,0:T(8,128)(2,1)S(1)}, bf16[16,64,128]{2,1,0:T(8,128)(2,1)S(1)}, u32[]{:S(2)}, u32[]{:S(2)}) collective-permute-start(bf16[16,64,128]{2,1,0:T(8,128)(2,1)S(1)} %join.10), channel_id=1, source_target_pairs={{0,224},{32,0},{64,32},{96,64},{128,96},{160,128},{192,160},{224,1... | collective-permute-start | bytes 786440 | tf_op jit(solution)/shard_map/ppermute | solution.py:420
  60.8 1.6 %collective-permute-start.4 = (bf16[128,2048]{1,0:T(8,128)(2,1)S(1)}, bf16[128,2048]{1,0:T(8,128)(2,1)S(1)}, u32[]{:S(2)}, u32[]{:S(2)}) collective-permute-start(bf16[128,2048]{1,0:T(8,128)(2,1)S(1)} %get-tuple-element.30), channel_id=1, source_target_pairs={{0,16},{4,20},{8,24},{12,28},{16,0},{20,4},{24,8},{28,12},{1,17},{... | collective-permute-start | bytes 1572872 | tf_op jit(solution)/shard_map/ppermute | solution.py:410
  62.5 3.8 %collective-permute-start.20 = (bf16[16,64,128]{2,1,0:T(8,128)(2,1)S(1)}, bf16[16,64,128]{2,1,0:T(8,128)(2,1)S(1)}, u32[]{:S(2)}, u32[]{:S(2)}) collective-permute-start(bf16[16,64,128]{2,1,0:T(8,128)(2,1)S(1)} %join.18), channel_id=1, source_target_pairs={{0,224},{32,0},{64,32},{96,64},{128,96},{160,128},{192,160},{224,1... | collective-permute-start | bytes 786440 | tf_op jit(solution)/shard_map/ppermute | solution.py:420
  66.4 1.1 %collective-permute-done.12.moving = bf16[16,64,128]{2,1,0:T(8,128)(2,1)S(1)} collective-permute-done((bf16[16,64,128]{2,1,0:T(8,128)(2,1)S(1)}, bf16[16,64,128]{2,1,0:T(8,128)(2,1)S(1)}, u32[]{:S(2)}, u32[]{:S(2)}) %collective-permute-start.12) | collective-permute-done | bytes 262176 | tf_op jit(solution)/shard_map/ppermute | solution.py:420
  68.1 3.8 %collective-permute-start.10 = (bf16[16,64,128]{2,1,0:T(8,128)(2,1)S(1)}, bf16[16,64,128]{2,1,0:T(8,128)(2,1)S(1)}, u32[]{:S(2)}, u32[]{:S(2)}) collective-permute-start(bf16[16,64,128]{2,1,0:T(8,128)(2,1)S(1)} %join.11), channel_id=1, source_target_pairs={{0,224},{32,0},{64,32},{96,64},{128,96},{160,128},{192,160},{224,1... | collective-permute-start | bytes 786440 | tf_op jit(solution)/shard_map/ppermute | solution.py:420
  71.9 1.8 %collective-permute-done.20.moving = bf16[16,64,128]{2,1,0:T(8,128)(2,1)S(1)} collective-permute-done((bf16[16,64,128]{2,1,0:T(8,128)(2,1)S(1)}, bf16[16,64,128]{2,1,0:T(8,128)(2,1)S(1)}, u32[]{:S(2)}, u32[]{:S(2)}) %collective-permute-start.20) | collective-permute-done | bytes 262176 | tf_op jit(solution)/shard_map/ppermute | solution.py:420
  73.7 3.8 %collective-permute-start.21 = (bf16[16,64,128]{2,1,0:T(8,128)(2,1)S(1)}, bf16[16,64,128]{2,1,0:T(8,128)(2,1)S(1)}, u32[]{:S(2)}, u32[]{:S(2)}) collective-permute-start(bf16[16,64,128]{2,1,0:T(8,128)(2,1)S(1)} %join.19), channel_id=1, source_target_pairs={{0,224},{32,0},{64,32},{96,64},{128,96},{160,128},{192,160},{224,1... | collective-permute-start | bytes 786440 | tf_op jit(solution)/shard_map/ppermute | solution.py:420
  77.7 2.5 %own.1.hole_own = f32[128,2048]{1,0:T(8,128)S(1)} custom-call(bf16[128,1024]{1,0:T(8,128)(2,1)} %hole_at.1, bf16[512,2048]{1,0:T(8,128)(2,1)S(1)} %get-tuple-element.29.line), custom_call_target="tpu_custom_call" | custom-call | flops 268435456 | bytes 4194304 | tf_op jit(solution)/shard_map/own/pallas_call | solution.py:282
  80.8 2.8 %collective-permute-done.21.high = bf16[16,64,128]{2,1,0:T(8,128)(2,1)S(1)} collective-permute-done((bf16[16,64,128]{2,1,0:T(8,128)(2,1)S(1)}, bf16[16,64,128]{2,1,0:T(8,128)(2,1)S(1)}, u32[]{:S(2)}, u32[]{:S(2)}) %collective-permute-start.21) | collective-permute-done | bytes 262176 | tf_op jit(solution)/shard_map/ppermute | solution.py:420
  83.6 1.6 %collective-permute-done.17.low = bf16[16,64,128]{2,1,0:T(8,128)(2,1)S(1)} collective-permute-done((bf16[16,64,128]{2,1,0:T(8,128)(2,1)S(1)}, bf16[16,64,128]{2,1,0:T(8,128)(2,1)S(1)}, u32[]{:S(2)}, u32[]{:S(2)}) %collective-permute-start.17) | collective-permute-done | bytes 262176 | tf_op jit(solution)/shard_map/ppermute | solution.py:420
  (46 shorter events, 5.9 us)
Async XLA Ops:
  1.1 15.3 %collective-permute-start.6 = (bf16[128,2048]{1,0:T(8,128)(2,1)S(1)}, bf16[128,2048]{1,0:T(8,128)(2,1)S(1)}, u32[]{:S(2)}, u32[]{:S(2)}) collective-permute-start(bf16[128,2048]{1,0:T(8,128)(2,1)S(1)} %shard_map.119.own), channel_id=1, source_target_pairs={{0,2},{1,3},{2,0},{3,1},{4,6},{5,7},{6,4},{7,5},{8,10},{9,11},{10,... | collective-permute-start | bytes 1572872 | tf_op jit(solution)/shard_map/ppermute | solution.py:389
  4.3 17.3 %collective-permute-start.5 = (bf16[128,2048]{1,0:T(8,128)(2,1)S(1)}, bf16[128,2048]{1,0:T(8,128)(2,1)S(1)}, u32[]{:S(2)}, u32[]{:S(2)}) collective-permute-start(bf16[128,2048]{1,0:T(8,128)(2,1)S(1)} %shard_map.119.own), channel_id=1, source_target_pairs={{0,1},{1,0},{2,3},{3,2},{4,5},{5,4},{6,7},{7,6},{8,9},{9,8},{10,11... | collective-permute-start | bytes 1572872 | tf_op jit(solution)/shard_map/ppermute | solution.py:390
  16.3 13.4 %collective-permute-start.7 = (bf16[128,2048]{1,0:T(8,128)(2,1)S(1)}, bf16[128,2048]{1,0:T(8,128)(2,1)S(1)}, u32[]{:S(2)}, u32[]{:S(2)}) collective-permute-start(bf16[128,2048]{1,0:T(8,128)(2,1)S(1)} %collective-permute-done.6.far), channel_id=1, source_target_pairs={{0,1},{1,0},{2,3},{3,2},{4,5},{5,4},{6,7},{7,6},{8,9},{9,8},{10,11... | collective-permute-start | bytes 1572872 | tf_op jit(solution)/shard_map/ppermute | solution.py:391
  17.4 26.9 %collective-permute-start.1 = (bf16[128,2048]{1,0:T(8,128)(2,1)S(1)}, bf16[128,2048]{1,0:T(8,128)(2,1)S(1)}, u32[]{:S(2)}, u32[]{:S(2)}) collective-permute-start(bf16[128,2048]{1,0:T(8,128)(2,1)S(1)} %get-tuple-element.28.block_0), channel_id=1, source_target_pairs={{0,12},{4,0},{8,4},{12,8},{16,28},{20,16},{24,20},{28,24},{1,13},{... | collective-permute-start | bytes 1572872 | tf_op jit(solution)/shard_map/ppermute | solution.py:393
  18.3 34.1 %collective-permute-start.2 = (bf16[128,2048]{1,0:T(8,128)(2,1)S(1)}, bf16[128,2048]{1,0:T(8,128)(2,1)S(1)}, u32[]{:S(2)}, u32[]{:S(2)}) collective-permute-start(bf16[128,2048]{1,0:T(8,128)(2,1)S(1)} %get-tuple-element.28.block_0), channel_id=1, source_target_pairs={{0,8},{4,12},{8,0},{12,4},{16,24},{20,28},{24,16},{28,20},{1,9},{5... | collective-permute-start | bytes 1572872 | tf_op jit(solution)/shard_map/ppermute | solution.py:394
  19.4 18.0 %collective-permute-start = (bf16[128,512]{1,0:T(8,128)(2,1)S(1)}, bf16[128,512]{1,0:T(8,128)(2,1)S(1)}, u32[]{:S(2)}, u32[]{:S(2)}) collective-permute-start(bf16[128,512]{1,0:T(8,128)(2,1)S(1)} %get-tuple-element.27), channel_id=1, source_target_pairs={{0,16},{4,20},{8,24},{12,28},{16,0},{20,4},{24,8},{28,12},{1,17},{... | collective-permute-start | bytes 393224 | tf_op jit(solution)/shard_map/ppermute | solution.py:395
  21.7 30.8 %collective-permute-start.3 = (bf16[128,2048]{1,0:T(8,128)(2,1)S(1)}, bf16[128,2048]{1,0:T(8,128)(2,1)S(1)}, u32[]{:S(2)}, u32[]{:S(2)}) collective-permute-start(bf16[128,2048]{1,0:T(8,128)(2,1)S(1)} %get-tuple-element.28.block_0), channel_id=1, source_target_pairs={{0,4},{4,8},{8,12},{12,0},{16,20},{20,24},{24,28},{28,16},{1,5},{5... | collective-permute-start | bytes 1572872 | tf_op jit(solution)/shard_map/ppermute | solution.py:392
  31.5 48.8 %copy-start.1 = (bf16[128,1,2048]{2,0,1:T(8,128)(2,1)S(1)}, bf16[128,1,2048]{2,0,1:T(8,128)(2,1)}, u32[]{:S(2)}) copy-start(bf16[128,1,2048]{2,0,1:T(8,128)(2,1)} %param.14) | copy-start | bytes 1572868
  31.5 48.8 %copy-start.2 = (s32[1,2048]{1,0:T(1,128)S(1)}, s32[1,2048]{1,0:T(1,128)}, u32[]{:S(2)}) copy-start(s32[1,2048]{1,0:T(1,128)} %gap_columns.1) | copy-start | bytes 24580
  31.5 14.7 %collective-permute-start.18 = (bf16[16,64,128]{2,1,0:T(8,128)(2,1)S(1)}, bf16[16,64,128]{2,1,0:T(8,128)(2,1)S(1)}, u32[]{:S(2)}, u32[]{:S(2)}) collective-permute-start(bf16[16,64,128]{2,1,0:T(8,128)(2,1)S(1)} %get-tuple-element.45), channel_id=1, source_target_pairs={{0,224},{32,0},{64,32},{96,64},{128,96},{160,128},{192,160},{224,1... | collective-permute-start | bytes 786440 | tf_op jit(solution)/shard_map/ppermute | solution.py:420
  37.4 12.8 %collective-permute-start.14 = (bf16[16,64,128]{2,1,0:T(8,128)(2,1)S(1)}, bf16[16,64,128]{2,1,0:T(8,128)(2,1)S(1)}, u32[]{:S(2)}, u32[]{:S(2)}) collective-permute-start(bf16[16,64,128]{2,1,0:T(8,128)(2,1)S(1)} %get-tuple-element.41), channel_id=1, source_target_pairs={{0,32},{32,64},{64,96},{96,128},{128,160},{160,192},{192,224},{224... | collective-permute-start | bytes 786440 | tf_op jit(solution)/shard_map/ppermute | solution.py:420
  44.3 13.0 %collective-permute-start.11 = (bf16[16,64,128]{2,1,0:T(8,128)(2,1)S(1)}, bf16[16,64,128]{2,1,0:T(8,128)(2,1)S(1)}, u32[]{:S(2)}, u32[]{:S(2)}) collective-permute-start(bf16[16,64,128]{2,1,0:T(8,128)(2,1)S(1)} %get-tuple-element.36), channel_id=1, source_target_pairs={{0,32},{32,64},{64,96},{96,128},{128,160},{160,192},{192,224},{224... | collective-permute-start | bytes 786440 | tf_op jit(solution)/shard_map/ppermute | solution.py:420
  46.2 11.2 %collective-permute-start.8 = (bf16[16,64,128]{2,1,0:T(8,128)(2,1)S(1)}, bf16[16,64,128]{2,1,0:T(8,128)(2,1)S(1)}, u32[]{:S(2)}, u32[]{:S(2)}) collective-permute-start(bf16[16,64,128]{2,1,0:T(8,128)(2,1)S(1)} %get-tuple-element.32), channel_id=1, source_target_pairs={{0,224},{32,0},{64,32},{96,64},{128,96},{160,128},{192,160},{224,1... | collective-permute-start | bytes 786440 | tf_op jit(solution)/shard_map/ppermute | solution.py:420
  50.2 12.2 %collective-permute-start.19 = (bf16[16,64,128]{2,1,0:T(8,128)(2,1)S(1)}, bf16[16,64,128]{2,1,0:T(8,128)(2,1)S(1)}, u32[]{:S(2)}, u32[]{:S(2)}) collective-permute-start(bf16[16,64,128]{2,1,0:T(8,128)(2,1)S(1)} %join.17), channel_id=1, source_target_pairs={{0,224},{32,0},{64,32},{96,64},{128,96},{160,128},{192,160},{224,1... | collective-permute-start | bytes 786440 | tf_op jit(solution)/shard_map/ppermute | solution.py:420
  52.4 13.9 %collective-permute-start.15 = (bf16[16,64,128]{2,1,0:T(8,128)(2,1)S(1)}, bf16[16,64,128]{2,1,0:T(8,128)(2,1)S(1)}, u32[]{:S(2)}, u32[]{:S(2)}) collective-permute-start(bf16[16,64,128]{2,1,0:T(8,128)(2,1)S(1)} %join.14), channel_id=1, source_target_pairs={{0,32},{32,64},{64,96},{96,128},{128,160},{160,192},{192,224},{224... | collective-permute-start | bytes 786440 | tf_op jit(solution)/shard_map/ppermute | solution.py:420
  57.3 10.2 %collective-permute-start.12 = (bf16[16,64,128]{2,1,0:T(8,128)(2,1)S(1)}, bf16[16,64,128]{2,1,0:T(8,128)(2,1)S(1)}, u32[]{:S(2)}, u32[]{:S(2)}) collective-permute-start(bf16[16,64,128]{2,1,0:T(8,128)(2,1)S(1)} %join.12), channel_id=1, source_target_pairs={{0,32},{32,64},{64,96},{96,128},{128,160},{160,192},{192,224},{224... | collective-permute-start | bytes 786440 | tf_op jit(solution)/shard_map/ppermute | solution.py:420
  57.5 10.5 %collective-permute-start.9 = (bf16[16,64,128]{2,1,0:T(8,128)(2,1)S(1)}, bf16[16,64,128]{2,1,0:T(8,128)(2,1)S(1)}, u32[]{:S(2)}, u32[]{:S(2)}) collective-permute-start(bf16[16,64,128]{2,1,0:T(8,128)(2,1)S(1)} %join.10), channel_id=1, source_target_pairs={{0,224},{32,0},{64,32},{96,64},{128,96},{160,128},{192,160},{224,1... | collective-permute-start | bytes 786440 | tf_op jit(solution)/shard_map/ppermute | solution.py:420
  60.8 19.4 %collective-permute-start.4 = (bf16[128,2048]{1,0:T(8,128)(2,1)S(1)}, bf16[128,2048]{1,0:T(8,128)(2,1)S(1)}, u32[]{:S(2)}, u32[]{:S(2)}) collective-permute-start(bf16[128,2048]{1,0:T(8,128)(2,1)S(1)} %get-tuple-element.30), channel_id=1, source_target_pairs={{0,16},{4,20},{8,24},{12,28},{16,0},{20,4},{24,8},{28,12},{1,17},{... | collective-permute-start | bytes 1572872 | tf_op jit(solution)/shard_map/ppermute | solution.py:410
  62.5 11.2 %collective-permute-start.20 = (bf16[16,64,128]{2,1,0:T(8,128)(2,1)S(1)}, bf16[16,64,128]{2,1,0:T(8,128)(2,1)S(1)}, u32[]{:S(2)}, u32[]{:S(2)}) collective-permute-start(bf16[16,64,128]{2,1,0:T(8,128)(2,1)S(1)} %join.18), channel_id=1, source_target_pairs={{0,224},{32,0},{64,32},{96,64},{128,96},{160,128},{192,160},{224,1... | collective-permute-start | bytes 786440 | tf_op jit(solution)/shard_map/ppermute | solution.py:420
  66.3 11.2 %collective-permute-start.16 = (bf16[16,64,128]{2,1,0:T(8,128)(2,1)S(1)}, bf16[16,64,128]{2,1,0:T(8,128)(2,1)S(1)}, u32[]{:S(2)}, u32[]{:S(2)}) collective-permute-start(bf16[16,64,128]{2,1,0:T(8,128)(2,1)S(1)} %join.15), channel_id=1, source_target_pairs={{0,32},{32,64},{64,96},{96,128},{128,160},{160,192},{192,224},{224... | collective-permute-start | bytes 786440 | tf_op jit(solution)/shard_map/ppermute | solution.py:420
  67.6 12.6 %collective-permute-start.13 = (bf16[16,64,128]{2,1,0:T(8,128)(2,1)S(1)}, bf16[16,64,128]{2,1,0:T(8,128)(2,1)S(1)}, u32[]{:S(2)}, u32[]{:S(2)}) collective-permute-start(bf16[16,64,128]{2,1,0:T(8,128)(2,1)S(1)} %join.13), channel_id=1, source_target_pairs={{0,32},{32,64},{64,96},{96,128},{128,160},{160,192},{192,224},{224... | collective-permute-start | bytes 786440 | tf_op jit(solution)/shard_map/ppermute | solution.py:420
  68.1 12.1 %collective-permute-start.10 = (bf16[16,64,128]{2,1,0:T(8,128)(2,1)S(1)}, bf16[16,64,128]{2,1,0:T(8,128)(2,1)S(1)}, u32[]{:S(2)}, u32[]{:S(2)}) collective-permute-start(bf16[16,64,128]{2,1,0:T(8,128)(2,1)S(1)} %join.11), channel_id=1, source_target_pairs={{0,224},{32,0},{64,32},{96,64},{128,96},{160,128},{192,160},{224,1... | collective-permute-start | bytes 786440 | tf_op jit(solution)/shard_map/ppermute | solution.py:420
  73.7 9.9 %collective-permute-start.21 = (bf16[16,64,128]{2,1,0:T(8,128)(2,1)S(1)}, bf16[16,64,128]{2,1,0:T(8,128)(2,1)S(1)}, u32[]{:S(2)}, u32[]{:S(2)}) collective-permute-start(bf16[16,64,128]{2,1,0:T(8,128)(2,1)S(1)} %join.19), channel_id=1, source_target_pairs={{0,224},{32,0},{64,32},{96,64},{128,96},{160,128},{192,160},{224,1... | collective-permute-start | bytes 786440 | tf_op jit(solution)/shard_map/ppermute | solution.py:420
  77.6 7.7 %collective-permute-start.17 = (bf16[16,64,128]{2,1,0:T(8,128)(2,1)S(1)}, bf16[16,64,128]{2,1,0:T(8,128)(2,1)S(1)}, u32[]{:S(2)}, u32[]{:S(2)}) collective-permute-start(bf16[16,64,128]{2,1,0:T(8,128)(2,1)S(1)} %join.16), channel_id=1, source_target_pairs={{0,32},{32,64},{64,96},{96,128},{128,160},{160,192},{192,224},{224... | collective-permute-start | bytes 786440 | tf_op jit(solution)/shard_map/ppermute | solution.py:420
  (2 other events, 54.7 us)
